TPU v7x, 256 devices: a whole 4x4x8 slice. The times are simulated.
256 devices in a mesh: aln: 8 (over x, core), seq: 32 (over z, y).
Axes of the slice: x: 4, y: 4, z: 8, core: 2. Of those that a mesh axis runs over, the one named last changes fastest.
Arguments:
- embedded_homologs: bfloat16 [2048, 128, 768], P(('aln', 'seq')), parts along dimension 0, may hold values from -6 to 6
- homolog_tallies: int32 [8], P('aln'), parts along dimension 0, may hold values from 64 to 256
- horizontal_probe_matrix: bfloat16 [768, 768], replicated
- horizontal_lookup_matrix: bfloat16 [768, 768], replicated
- horizontal_content_matrix: bfloat16 [768, 768], replicated, may hold values from -0.21875 to 0.21875
- vertical_probe_matrix: bfloat16 [768, 768], replicated
- vertical_lookup_matrix: bfloat16 [768, 768], replicated
- vertical_content_matrix: bfloat16 [768, 768], replicated, may hold values from -0.21875 to 0.21875
Outputs:
- row_output: bfloat16 [2048, 128, 768], P(('aln', 'seq')), parts along dimension 0
- column_output: bfloat16 [2048, 128, 768], P(('aln', 'seq')), parts along dimension 0
There are 8 independent parts, one for each index of `aln`. A program takes and returns all parts, laid end to end along the dimension named above; an argument that names none is the same for every part. Nothing has to cross between parts.
Inputs may be any that keep to these rules, and one draw needn't show every extreme that they name: Sequence slots from homolog_tallies[0] on are padding.
All inputs are finite; a program needn't handle non-finite values.
Results may differ from a plain program's by a relative error of at most 0.024.
Values may be sent and summed in bfloat16 or wider, within the bound.
No kernel may reach another device: no remote copies, remote signals or barrier semaphores. Data moves between devices by JAX's collectives and lax.ppermute only.
A program may use at most 128 MiB of HBM per device.

v0:
```python
import jax
import jax.numpy as jnp
from jax import lax
from jax.sharding import Mesh
from jax.sharding import PartitionSpec as P

H = 12
DH = 64
SEQ = ("seq_0", "seq_1")
ALN_SEQ = ("aln", "seq_0", "seq_1")


def split_up(x, dim, count):
    lengths = x.shape
    tiles = x.reshape(*lengths[:dim], count, lengths[dim] // count, *lengths[dim + 1 :])
    return jnp.moveaxis(tiles, dim, 0)


def summed_on_arrival(x, axis, dim):
    tiles = split_up(x, dim, lax.axis_size(axis))
    arrived = lax.all_to_all(tiles, axis, split_axis=0, concat_axis=0, tiled=True)
    return arrived.astype(jnp.float32).sum(axis=0)


def gathered_by_axis(x, axes, dim):
    for axis in reversed(axes):
        x = lax.all_gather(x, axis, axis=dim, tiled=True)
    return x


def exchange_in_groups(x, axis, split_dim, concat_dim, work, item_dim, out_dim):
    items = jax.tree.leaves(x)[0].shape[item_dim]
    count = 2 if items % 2 == 0 else 1
    gathered = []
    for k in range(count):
        group = jax.tree.map(
            lambda a: lax.slice_in_dim(
                a, k * (items // count), (k + 1) * (items // count), axis=item_dim
            ),
            x,
        )
        gathered.append(
            work(
                lax.all_to_all(
                    group, axis, split_axis=split_dim, concat_axis=concat_dim, tiled=True
                )
            )
        )
    return jax.tree.map(lambda *parts: jnp.concatenate(parts, axis=out_dim), *gathered)


def standardize_features(values):
    centre = jnp.mean(values, axis=-1, keepdims=True)
    spread = jnp.mean((values - centre) ** 2, axis=-1, keepdims=True)
    return (values - centre) * lax.rsqrt(spread + 1e-05)


def project(standardized_activations, weight):
    lead = standardized_activations.shape[:-1]
    flat = standardized_activations.reshape(-1, standardized_activations.shape[-1])
    result = jnp.dot(flat, weight, preferred_element_type=jnp.float32).astype(jnp.bfloat16)
    return result.reshape(lead + (H, DH))


def column_attend(query, key_rows, value_rows, live_all):
    scores = jnp.einsum(
        "schd,tchd->chst", query, key_rows, preferred_element_type=jnp.float32
    ) / jnp.sqrt(jnp.float32(DH))
    scores = jnp.where(live_all[None, None, None, :] > 0, scores, jnp.float32(-1e30))
    weights = jax.nn.softmax(scores, axis=-1).astype(jnp.bfloat16)
    result = jnp.einsum("chst,tchd->schd", weights, value_rows, preferred_element_type=jnp.float32)
    result = (result * live_all[:, None, None, None]).astype(jnp.bfloat16)
    return result.reshape(result.shape[0], 1, result.shape[1], H * DH)


def local(
    embedded_homologs,
    homolog_tallies,
    horizontal_probe_matrix,
    horizontal_lookup_matrix,
    horizontal_content_matrix,
    vertical_probe_matrix,
    vertical_lookup_matrix,
    vertical_content_matrix,
):
    homolog_capacity = embedded_homologs.shape[0]
    position_total = embedded_homologs.shape[1]
    embed_dimension = embedded_homologs.shape[2]
    groups = lax.axis_size(SEQ)
    count = homolog_tallies[0]
    first = lax.axis_index(SEQ) * homolog_capacity
    livef = (first + jnp.arange(homolog_capacity, dtype=jnp.int32) < count).astype(jnp.float32)
    standardized_activations = standardize_features(embedded_homologs.astype(jnp.float32)).astype(
        jnp.bfloat16
    )
    rq = project(standardized_activations, horizontal_probe_matrix)
    rk = project(standardized_activations, horizontal_lookup_matrix)
    rv = project(standardized_activations, horizontal_content_matrix)
    masked = rq * livef.astype(jnp.bfloat16)[:, None, None, None]
    partial_value = jnp.einsum("sihd,sjhd->hij", masked, rk, preferred_element_type=jnp.float32)
    scale = jnp.sqrt(jnp.float32(DH)) * jnp.sqrt(count.astype(jnp.float32))
    shares = summed_on_arrival(partial_value.astype(jnp.bfloat16), SEQ, 1) / scale
    share_weights = jax.nn.softmax(shares, axis=-1).astype(jnp.bfloat16)
    weights = gathered_by_axis(share_weights, SEQ, 1)
    horizontal_mixing_result = jnp.einsum(
        "hij,sjhd->sihd", weights, rv, preferred_element_type=jnp.float32
    )
    horizontal_mixing_result = (
        (horizontal_mixing_result * livef[:, None, None, None])
        .astype(jnp.bfloat16)
        .reshape(homolog_capacity, position_total, embed_dimension)
    )
    intermediate_activations = embedded_homologs.astype(
        jnp.float32
    ) + horizontal_mixing_result.astype(jnp.float32)
    normed2 = standardize_features(intermediate_activations).astype(jnp.bfloat16)
    per_group = position_total // groups
    blocks = normed2.reshape(homolog_capacity, groups, per_group, embed_dimension)

    def attend_normed(block):
        total = block.shape[0]
        live_all = (jnp.arange(total, dtype=jnp.int32) < count).astype(jnp.float32)
        rows = block.reshape(total, block.shape[2], embed_dimension)
        return column_attend(
            project(rows, vertical_probe_matrix),
            project(rows, vertical_lookup_matrix),
            project(rows, vertical_content_matrix),
            live_all,
        )

    gathered = exchange_in_groups(blocks, SEQ, 1, 0, attend_normed, 2, 2)
    returned = lax.all_to_all(gathered, SEQ, split_axis=0, concat_axis=1, tiled=True)
    column_out = returned.reshape(homolog_capacity, position_total, embed_dimension)
    return (horizontal_mixing_result, column_out)


def solution(mesh):
    split = Mesh(mesh.devices.reshape(mesh.shape["aln"], 8, 4), ("aln", "seq_0", "seq_1"))
    in_specs = (P(ALN_SEQ, None, None), P("aln"), P(), P(), P(), P(), P(), P())
    out_specs = (P(ALN_SEQ, None, None), P(ALN_SEQ, None, None))
    return jax.shard_map(local, mesh=split, in_specs=in_specs, out_specs=out_specs, check_vma=False)
```

profile of v0, /device:TPU:4, one launch (start us, length us, event | category | flops | bytes accessed | tf_op | source)
XLA Modules:
  0.0 230.9 jit_solution(3595680037346730867)
XLA Ops:
  10.5 3.2 %copy.121 = bf16[96,8,8,128]{3,2,1,0:T(8,128)(2,1)} copy(bf16[96,8,8,128]{3,1,2,0:T(8,128)(2,1)} %bitcast.80) | data formatting | bytes 3145728
  18.8 3.0 %copy.122 = bf16[96,8,8,128]{3,2,1,0:T(8,128)(2,1)} copy(bf16[96,8,8,128]{3,1,2,0:T(8,128)(2,1)} %bitcast.81) | data formatting | bytes 3145728
  25.3 11.5 %all-to-all-start = ((bf16[32,12,4,128]{3,2,1,0:T(4,128)(2,1)}), bf16[32,12,4,128]{3,2,1,0:T(4,128)(2,1)S(1)}, u32[]{:S(2)}, u32[]{:S(2)}) async-start(bf16[32,12,4,128]{3,2,1,0:T(4,128)(2,1)} %bitcast.75), calls=%async_computation | async-start | bytes 786432 | tf_op jit(solution)/shard_map/all_to_all | solution.py:21
  36.9 4.3 %convolution_convert_fusion.2 = bf16[1024,768]{1,0:T(8,128)(2,1)} fusion(bf16[1024,768]{1,0:T(8,128)(2,1)} %bitcast.89, bf16[768,768]{1,0:T(8,128)(2,1)} %param.12), kind=kOutput, calls=%fused_computation.33 | convolution fusion | flops 1208745984 | bytes 4325376 | tf_op jit(solution)/shard_map/dot_general | solution.py:61
  43.7 3.0 %copy.120 = bf16[96,8,8,128]{3,2,1,0:T(8,128)(2,1)} copy(bf16[96,8,8,128]{3,1,2,0:T(8,128)(2,1)} %bitcast.82) | data formatting | bytes 3145728
  46.7 5.4 %all-to-all-done = bf16[32,12,4,128]{3,2,1,0:T(4,128)(2,1)S(1)} async-done(((bf16[32,12,4,128]{3,2,1,0:T(4,128)(2,1)}), bf16[32,12,4,128]{3,2,1,0:T(4,128)(2,1)S(1)}, u32[]{:S(2)}, u32[]{:S(2)}) %all-to-all-start) | async-done | bytes 393248 | tf_op jit(solution)/shard_map/all_to_all | solution.py:21
  52.6 11.9 %all_gather.6 = bf16[12,16,128]{2,0,1:T(8,128)(2,1)S(1)} all-gather(bf16[12,4,128]{2,0,1:T(8,128)(2,1)S(1)} %copy.94), channel_id=1, replica_groups=mesh['aln'=8,'seq_0'=8,'seq_1'=4] {'seq_1'}, dimensions={1}, use_global_device_ids=true | all-gather | bytes 61440 | tf_op jit(solution)/shard_map/all_gather | solution.py:27
  64.5 25.4 %all_gather.7 = bf16[12,128,128]{2,1,0:T(8,128)(2,1)S(1)} all-gather(bf16[12,16,128]{2,1,0:T(8,128)(2,1)S(1)} %copy.95), channel_id=1, replica_groups=mesh['aln'=8,'seq_0'=8,'seq_1'=4] {'seq_0'}, dimensions={1}, use_global_device_ids=true | all-gather | bytes 442368 | tf_op jit(solution)/shard_map/all_gather | solution.py:27
  100.9 20.8 %all_to_all.50 = bf16[8,32,2,768]{3,0,2,1:T(8,128)(2,1)S(1)} all-to-all(bf16[8,32,2,768]{3,0,2,1:T(8,128)(2,1)S(1)} %get-tuple-element.12), channel_id=1, replica_groups=mesh['aln'=8,'seq_0'=8,'seq_1'=4] {'seq_0','seq_1'}, dimensions={1} | all-to-all | bytes 1572864 | tf_op jit(solution)/shard_map/all_to_all | solution.py:44
  121.7 6.1 %all-to-all-start.2 = ((bf16[8,32,2,768]{3,0,2,1:T(8,128)(2,1)}), bf16[8,32,2,768]{3,0,2,1:T(8,128)(2,1)S(1)}, u32[]{:S(2)}, u32[]{:S(2)}) async-start(bf16[8,32,2,768]{3,0,2,1:T(8,128)(2,1)} %get-tuple-element.13), calls=%async_computation.2 | async-start | bytes 1572864 | tf_op jit(solution)/shard_map/all_to_all | solution.py:44
  128.7 3.1 %convolution_convert_fusion.7 = bf16[512,768]{1,0:T(8,128)(2,1)} fusion(bf16[512,768]{1,0:T(8,128)(2,1)S(1)} %reshape_reshape.4, bf16[768,768]{1,0:T(8,128)(2,1)} %param.13), kind=kOutput, calls=%fused_computation.54 | convolution fusion | flops 604372992 | bytes 2752512 | tf_op jit(solution)/shard_map/dot_general | solution.py:61
  133.4 10.1 %all-to-all-done.2 = bf16[8,32,2,768]{3,0,2,1:T(8,128)(2,1)S(1)} async-done(((bf16[8,32,2,768]{3,0,2,1:T(8,128)(2,1)}), bf16[8,32,2,768]{3,0,2,1:T(8,128)(2,1)S(1)}, u32[]{:S(2)}, u32[]{:S(2)}) %all-to-all-start.2) | async-done | bytes 786464 | tf_op jit(solution)/shard_map/all_to_all | solution.py:44
  144.5 3.0 %convolution_convert_fusion.4 = bf16[512,768]{1,0:T(8,128)(2,1)} fusion(bf16[512,768]{1,0:T(8,128)(2,1)S(1)} %reshape_reshape.5, bf16[768,768]{1,0:T(8,128)(2,1)} %param.13), kind=kOutput, calls=%fused_computation.51 | convolution fusion | flops 604372992 | bytes 2752512 | tf_op jit(solution)/shard_map/dot_general | solution.py:61
  152.6 2.8 %reshape.116 = bf16[256,2,12,64]{3,2,1,0:T(8,128)(2,1)S(1)} reshape(bf16[512,768]{1,0:T(8,128)(2,1)} %convolution_convert_fusion.7) | data formatting | bytes 1572864 | tf_op jit(solution)/shard_map/reshape | solution.py:62
  157.7 3.8 %reshape.115 = bf16[256,2,12,64]{3,2,1,0:T(8,128)(2,1)} reshape(bf16[512,768]{1,0:T(8,128)(2,1)} %convolution_convert_fusion.8) | data formatting | bytes 1572864 | tf_op jit(solution)/shard_map/reshape | solution.py:62
  161.5 2.9 %fusion.24 = f32[2,12,256,256]{2,3,1,0:T(8,128)S(1)} fusion(bf16[256,2,12,64]{3,2,1,0:T(8,128)(2,1)} %reshape.117, bf16[256,2,12,64]{3,2,1,0:T(8,128)(2,1)S(1)} %reshape.116), kind=kOutput, calls=%fused_computation.41 | convolution fusion | flops 201326592 | bytes 7864320 | tf_op jit(solution)/shard_map/schd,tchd->chst/dot_general | solution.py:66
  171.7 2.7 %reshape.120 = bf16[256,2,12,64]{3,2,1,0:T(8,128)(2,1)S(1)} reshape(bf16[512,768]{1,0:T(8,128)(2,1)} %convolution_convert_fusion.4) | data formatting | bytes 1572864 | tf_op jit(solution)/shard_map/reshape | solution.py:62
  174.5 3.8 %reshape.121 = bf16[256,2,12,64]{3,2,1,0:T(8,128)(2,1)} reshape(bf16[512,768]{1,0:T(8,128)(2,1)} %convolution_convert_fusion.3) | data formatting | bytes 1572864 | tf_op jit(solution)/shard_map/reshape | solution.py:62
  178.2 2.9 %fusion.20 = f32[2,12,256,256]{2,3,1,0:T(8,128)S(1)} fusion(bf16[256,2,12,64]{3,2,1,0:T(8,128)(2,1)} %reshape.121, bf16[256,2,12,64]{3,2,1,0:T(8,128)(2,1)S(1)} %reshape.120), kind=kOutput, calls=%fused_computation.37 | convolution fusion | flops 201326592 | bytes 7864320 | tf_op jit(solution)/shard_map/schd,tchd->chst/dot_general | solution.py:66
  181.1 4.5 %fusion.55 = (f32[2,12,256]{2,1,0:T(8,128)S(1)}, f32[2,12,256,256]{2,3,1,0:T(8,128)}) fusion(f32[2,12,256,256]{2,3,1,0:T(8,128)S(1)} %fusion.20, pred[256]{0:T(512)(128)(4,1)S(1)} %get-tuple-element.21), kind=kOutput, calls=%fused_computation.81 | output fusion | flops 9437439 | bytes 12607744 | tf_op jit(solution)/shard_map/sub | solution.py:70
  185.6 2.7 %reshape.119 = bf16[256,2,12,64]{3,2,1,0:T(8,128)(2,1)S(1)} reshape(bf16[512,768]{1,0:T(8,128)(2,1)} %convolution_convert_fusion.5) | data formatting | bytes 1572864 | tf_op jit(solution)/shard_map/reshape | solution.py:62
  188.3 4.8 %multiply_convert_fusion.2 = bf16[2,12,64,256]{3,2,1,0:T(8,128)(2,1)} fusion(f32[2,12,256,256]{2,3,1,0:T(8,128)} %get-tuple-element.17, f32[2,12,256]{2,1,0:T(8,128)S(1)} %get-tuple-element.16, bf16[256,2,12,64]{3,2,1,0:T(8,128)(2,1)S(1)} %reshape.119, f32[256]{0:T(256)S(1)} %get-tuple-element.20), kind=kOutput, calls=%fused_computation.45 | convolution fusion | flops 205258752 | bytes 7889920 | tf_op jit(solution)/shard_map/chst,tchd->schd/dot_general | solution.py:71
  193.1 2.7 %copy.111 = bf16[256,1,2,768]{3,2,1,0:T(2,128)(2,1)S(1)} copy(bf16[256,1,2,768]{0,3,2,1:T(8,128)(2,1)} %bitcast.94) | data formatting | bytes 1572864 | tf_op jit(solution)/shard_map/reshape | solution.py:73
  197.5 31.6 %all_to_all.51 = bf16[256,1,4,768]{3,2,1,0:T(4,128)(2,1)S(1)} all-to-all(bf16[256,1,4,768]{3,2,1,0:T(4,128)(2,1)S(1)} %pad_maximum_fusion), channel_id=1, replica_groups=mesh['aln'=8,'seq_0'=8,'seq_1'=4] {'seq_0','seq_1'}, dimensions={0} | all-to-all | bytes 3145728 | tf_op jit(solution)/shard_map/all_to_all | solution.py:132
  (69 shorter events, 53.3 us)
Async XLA Ops:
  0.6 4.8 %copy-start = (bf16[768,768]{1,0:T(8,128)(2,1)S(1)}, bf16[768,768]{1,0:T(8,128)(2,1)}, u32[]{:S(2)}) copy-start(bf16[768,768]{1,0:T(8,128)(2,1)} %param.10) | copy-start | bytes 3538948
  0.6 2.5 %copy-start.2 = (bf16[8,128,768]{2,1,0:T(8,128)(2,1)S(1)}, bf16[8,128,768]{2,1,0:T(8,128)(2,1)}, u32[]{:S(2)}) copy-start(bf16[8,128,768]{2,1,0:T(8,128)(2,1)} %param.8) | copy-start | bytes 4718596
  4.2 1.1 copy-start.5
  10.5 3.2 %copy-start.6 = (bf16[8,128,768]{2,1,0:T(8,128)(2,1)S(1)}, bf16[8,128,768]{2,1,0:T(8,128)(2,1)}, u32[]{:S(2)}) copy-start(bf16[8,128,768]{2,1,0:T(8,128)(2,1)} %copy-done.5) | copy-start | bytes 4718596
  10.5 3.2 %copy-start.8 = (bf16[768,768]{1,0:T(8,128)(2,1)S(1)}, bf16[768,768]{1,0:T(8,128)(2,1)}, u32[]{:S(2)}) copy-start(bf16[768,768]{1,0:T(8,128)(2,1)} %param.11) | copy-start | bytes 3538948
  25.3 26.8 %all-to-all-start = ((bf16[32,12,4,128]{3,2,1,0:T(4,128)(2,1)}), bf16[32,12,4,128]{3,2,1,0:T(4,128)(2,1)S(1)}, u32[]{:S(2)}, u32[]{:S(2)}) async-start(bf16[32,12,4,128]{3,2,1,0:T(4,128)(2,1)} %bitcast.75), calls=%async_computation | async-start | bytes 786432 | tf_op jit(solution)/shard_map/all_to_all | solution.py:21
  95.7 2.0 copy-start.3
  121.7 21.9 %all-to-all-start.2 = ((bf16[8,32,2,768]{3,0,2,1:T(8,128)(2,1)}), bf16[8,32,2,768]{3,0,2,1:T(8,128)(2,1)S(1)}, u32[]{:S(2)}, u32[]{:S(2)}) async-start(bf16[8,32,2,768]{3,0,2,1:T(8,128)(2,1)} %get-tuple-element.13), calls=%async_computation.2 | async-start | bytes 1572864 | tf_op jit(solution)/shard_map/all_to_all | solution.py:44
  128.7 3.1 %copy-start.9 = (bf16[768,768]{1,0:T(8,128)(2,1)S(1)}, bf16[768,768]{1,0:T(8,128)(2,1)}, u32[]{:S(2)}) copy-start(bf16[768,768]{1,0:T(8,128)(2,1)} %param.14) | copy-start | bytes 3538948
  144.5 3.0 %copy-start.10 = (bf16[768,768]{1,0:T(8,128)(2,1)S(1)}, bf16[768,768]{1,0:T(8,128)(2,1)}, u32[]{:S(2)}) copy-start(bf16[768,768]{1,0:T(8,128)(2,1)} %param.14) | copy-start | bytes 3538948
  147.6 1.7 copy-start.11
  152.6 2.8 %copy-start.7 = (bf16[512,768]{1,0:T(8,128)(2,1)S(1)}, bf16[512,768]{1,0:T(8,128)(2,1)}, u32[]{:S(2)}) copy-start(bf16[512,768]{1,0:T(8,128)(2,1)} %convolution_convert_fusion.6) | copy-start | bytes 2359300
  164.3 2.6 %copy-start.4 = (bf16[256,2,12,64]{3,2,1,0:T(8,128)(2,1)S(1)}, bf16[256,2,12,64]{3,2,1,0:T(8,128)(2,1)}, u32[]{:S(2)}) copy-start(bf16[256,2,12,64]{3,2,1,0:T(8,128)(2,1)} %reshape.115) | copy-start | bytes 2359300
  229.5 1.4 copy-start.1
where the time goes:
time: 232 us; the launch traced here: 231 us
  blocking collectives  89.6 us (39%)
  local copies, waits for them, and re-layouts  51.6 us (22%)
  matrix products  39.5 us (17%)
  starting transfers between devices  17.6 us (8%)
  waiting for transfers between devices  15.5 us (7%)
  other arithmetic  15.2 us (7%)
    all_gather x2, blocking collectives, gathered_by_axis(): x = lax.all_gather(x, axis, axis=dim, tiled=True)  37.3 us
    all_to_all x1, blocking collectives, local(): lax.all_to_all(gathered, SEQ, split_axis=0, concat_axis=1, tiled=True)  31.6 us
    dot_general x9, matrix products, project(): jnp.dot(flat, weight, preferred_element_type=jnp.float32)  22.1 us
    all_to_all x1, blocking collectives, exchange_in_groups(): lax.all_to_all(group, axis, split_axis=split_dim, concat_axis=concat_dim,...  20.8 us
    reshape x6, local copies, waits for them, and re-layouts, project(): return result.reshape(lead + (H, DH))  18.1 us
    unnamed x29, local copies, waits for them, and re-layouts  14.4 us
    all_to_all x1, starting transfers between devices, summed_on_arrival(): lax.all_to_all(tiles, axis, split_axis=0, concat_axis=0, tiled=True)  11.5 us
    all_to_all x1, waiting for transfers between devices, exchange_in_groups(): lax.all_to_all(group, axis, split_axis=split_dim, concat_axis=concat_dim,...  10.1 us
  transfers between devices with their start and end apart: 2, of which 2 were waited for; matrix products, arithmetic and copies ran while one was open for 7% of the time, Pallas kernels for 0%

commit v1 on v0

v1 whole, which is shorter than its diff:
```python
import functools
import math

import jax
import jax.numpy as jnp
from jax import lax
from jax.experimental import pallas as pl
from jax.experimental.pallas import tpu as pltpu
from jax.sharding import PartitionSpec as P

H = 12
DH = 64
SEQ = "seq"
LANES = 128
EPS = 1e-05
BF16 = jnp.bfloat16
F32 = jnp.float32
NT = (((1,), (1,)), ((), ()))


def standardize(values):
    centre = jnp.mean(values, axis=-1, keepdims=True)
    shifted = values - centre
    spread = jnp.mean(shifted * shifted, axis=-1, keepdims=True)
    return shifted * lax.rsqrt(spread + EPS)


def half_masks():
    lane = lax.broadcasted_iota(jnp.int32, (1, LANES), 1)
    low = (lane < DH).astype(F32)
    return low.astype(BF16), (1.0 - low).astype(BF16)


def lane_block(value, index):
    return value[:, index * LANES : (index + 1) * LANES]


def logits_kernel(meta, x_ref, wq_ref, wk_ref, normed_ref, logits_ref, total):
    step = pl.program_id(0)
    rows = x_ref.shape[0] // 2
    first, count = meta[0], meta[1]
    normed = standardize(x_ref[...].astype(F32)).astype(BF16)
    normed_ref[...] = normed
    row = lax.broadcasted_iota(jnp.int32, (2 * rows, 1), 0)
    sequence = first + 2 * step + (row >= rows).astype(jnp.int32)
    live = (sequence < count).astype(F32)
    q = (jnp.dot(normed, wq_ref[...], preferred_element_type=F32) * live).astype(BF16)
    k = jnp.dot(normed, wk_ref[...], preferred_element_type=F32).astype(BF16)
    low, high = half_masks()

    @pl.when(step == 0)
    def _():
        total[...] = jnp.zeros_like(total)

    for pair in range(H // 2):
        qp, kp = lane_block(q, pair), lane_block(k, pair)
        both = jnp.concatenate([qp[:rows], qp[rows:]], axis=1)
        even = jnp.concatenate([kp[:rows] * low, kp[rows:] * low], axis=1)
        odd = jnp.concatenate([kp[:rows] * high, kp[rows:] * high], axis=1)
        keys = jnp.concatenate([even, odd], axis=0)
        got = lax.dot_general(both, keys, NT, preferred_element_type=F32)
        at = 2 * pair * rows
        total[at : at + rows, :] += got[:, :rows]
        total[at + rows : at + 2 * rows, :] += got[:, rows:]

    @pl.when(step == pl.num_programs(0) - 1)
    def _():
        logits_ref[...] = total[...].astype(BF16)


def weights_kernel(scale_ref, parts_ref, out_ref):
    logits = parts_ref[0].astype(F32)
    for source in range(1, parts_ref.shape[0]):
        logits += parts_ref[source].astype(F32)
    logits = logits * scale_ref[0]
    top = jnp.max(logits, axis=-1, keepdims=True)
    powers = jnp.exp(logits - top)
    weights = (powers / jnp.sum(powers, axis=-1, keepdims=True)).astype(BF16)
    for target in range(out_ref.shape[0]):
        out_ref[target] = weights


def mix_kernel(meta, w_ref, rv_ref, x_ref, row_ref, *rest):
    sends, held = rest[:-1], rest[-1]
    step = pl.program_id(0)
    rows = x_ref.shape[0] // 2
    first, count = meta[0], meta[1]
    low, high = half_masks()
    mixed = [[], []]
    for pair in range(H // 2):
        at = 2 * pair * rows
        weights = jnp.concatenate([w_ref[at : at + rows, :], w_ref[at + rows : at + 2 * rows, :]], axis=1)
        lanes = slice(pair * LANES, (pair + 1) * LANES)
        values = []
        for s in range(2):
            v = rv_ref[s * rows : (s + 1) * rows, lanes]
            values.append(jnp.concatenate([v * low, v * high], axis=0))
        got = jnp.dot(weights, jnp.concatenate(values, axis=1), preferred_element_type=F32)
        for s in range(2):
            mixed[s].append(lane_block(got, s))
    for s in range(2):
        live = (first + 2 * step + s < count).astype(F32)
        part = slice(s * rows, (s + 1) * rows)
        out = (jnp.concatenate(mixed[s], axis=1) * live).astype(BF16)
        row_ref[part, :] = out
        total = x_ref[part, :].astype(F32) + out.astype(F32)
        held[2 * step + s] = standardize(total)

    @pl.when(step == pl.num_programs(0) - 1)
    def _():
        each = rows // len(sends)
        size = 16
        for k, send in enumerate(sends):
            for block in range(each // size):
                start = k * each + block * size
                turned = jnp.swapaxes(held[:, start : start + size, :], 0, 1)
                flat = turned.reshape(size * held.shape[0], held.shape[2])
                span = size * held.shape[0]
                send[block * span : (block + 1) * span, :] = flat.astype(BF16)


def column_kernel(columns, meta, n_ref, wq_ref, wk_ref, wv_ref, out_ref):
    count = meta[1]
    rows = n_ref.shape[0]
    total = rows // columns
    width = wq_ref.shape[1]
    factor = math.log2(math.e) / math.sqrt(DH)
    n = n_ref[...]
    q = jnp.dot(n, wq_ref[...], preferred_element_type=F32) * factor
    k = jnp.dot(n, wk_ref[...], preferred_element_type=F32)
    v = jnp.dot(n, wv_ref[...], preferred_element_type=F32)
    lane = lax.broadcasted_iota(jnp.int32, (1, LANES), 1)
    low = lane < DH
    first_high = (lane == DH).astype(F32)
    first_low = (lane == 0).astype(F32)
    row = lax.broadcasted_iota(jnp.int32, (total, 1), 0)
    alive = row < count
    bias = jnp.where(alive, 0.0, -1e30).astype(F32)
    live = alive.astype(F32)

    def column(value, c):
        return value.reshape(total // 8, columns, 8, width)[:, c].reshape(total, width)

    results = []
    for c in range(columns):
        qc, kc, vc = column(q, c), column(k, c), column(v, c)
        pieces = []
        for pair in range(width // LANES):
            qp, kp, vp = lane_block(qc, pair), lane_block(kc, pair), lane_block(vc, pair)
            mixes = []
            for even in (True, False):
                if even:
                    qh = jnp.where(low, qp, first_high)
                    kh = jnp.where(low, kp, bias)
                    vh = jnp.where(low, vp, 1.0)
                else:
                    qh = jnp.where(low, first_low, qp)
                    kh = jnp.where(low, bias, kp)
                    vh = jnp.where(low, 1.0, vp)
                scores = lax.dot_general(
                    qh.astype(BF16), kh.astype(BF16), NT, preferred_element_type=F32
                )
                top = jnp.max(scores, axis=-1, keepdims=True)
                powers = jnp.exp2(scores - top).astype(BF16)
                mixes.append(jnp.dot(powers, vh.astype(BF16), preferred_element_type=F32))
            values = jnp.where(low, mixes[0], mixes[1])
            sums = jnp.where(low, mixes[1], mixes[0])
            pieces.append(values * (live / pltpu.roll(sums, DH, 1)))
        results.append(jnp.concatenate(pieces, axis=1))
    if columns > 1:
        stacked = jnp.stack([r.reshape(total // 8, 8, width) for r in results], axis=1)
    else:
        stacked = results[0]
    out_ref[...] = stacked.reshape(rows, width).astype(BF16)


def turn_kernel(recv_ref, out_ref):
    sequences, size = out_ref.shape[0], out_ref.shape[1]
    got = recv_ref[...].astype(F32).reshape(size, sequences, recv_ref.shape[1])
    out_ref[...] = jnp.swapaxes(got, 0, 1).astype(BF16)


def turn_into(recv_ref, kept_ref, out_ref):
    turn_kernel(recv_ref, out_ref)


def row_spec(rows, width):
    return pl.BlockSpec((rows, width), lambda i, *_: (i, 0))


def whole_spec(shape):
    return pl.BlockSpec(shape, lambda i, *_: (0,) * len(shape))


def call(kernel, meta, args, grid, in_specs, out_specs, out_shape, scratch, cost, name):
    return pl.pallas_call(
        kernel,
        grid_spec=pltpu.PrefetchScalarGridSpec(
            num_scalar_prefetch=1,
            grid=grid,
            in_specs=in_specs,
            out_specs=out_specs,
            scratch_shapes=scratch,
        ),
        out_shape=out_shape,
        cost_estimate=cost,
        compiler_params=pltpu.CompilerParams(dimension_semantics=("arbitrary",) * len(grid)),
        name=name,
    )(meta, *args)


CHUNKS = 2


def local(x, tallies, hq, hk, hv, vq, vk, vv):
    sequences, positions, width = x.shape
    groups = lax.axis_size(SEQ)
    tokens = sequences * positions
    count = tallies[0]
    meta = jnp.stack([lax.axis_index(SEQ) * sequences, count]).astype(jnp.int32)
    flat = x.reshape(tokens, width)
    step_rows = 2 * positions
    steps = tokens // step_rows
    share = H * positions // groups

    normed, logits = call(
        logits_kernel,
        meta,
        (flat, hq, hk),
        (steps,),
        [row_spec(step_rows, width), whole_spec((width, width)), whole_spec((width, width))],
        [row_spec(step_rows, width), whole_spec((H * positions, positions))],
        [
            jax.ShapeDtypeStruct((tokens, width), BF16),
            jax.ShapeDtypeStruct((H * positions, positions), BF16),
        ],
        [pltpu.VMEM((H * positions, positions), F32)],
        pl.CostEstimate(flops=4 * tokens * width * width, bytes_accessed=6 << 20, transcendentals=0),
        "row_logits",
    )
    parts = lax.all_to_all(
        logits.reshape(groups, share, positions), SEQ, split_axis=0, concat_axis=0, tiled=True
    )
    rv = jnp.dot(normed, hv, preferred_element_type=F32).astype(BF16)
    scale = (1.0 / (jnp.sqrt(F32(DH)) * jnp.sqrt(count.astype(F32)))).reshape(1)
    copies = pl.pallas_call(
        weights_kernel,
        in_specs=[
            pl.BlockSpec(memory_space=pltpu.SMEM),
            pl.BlockSpec(memory_space=pltpu.VMEM),
        ],
        out_specs=pl.BlockSpec(memory_space=pltpu.VMEM),
        out_shape=jax.ShapeDtypeStruct((groups, share, positions), BF16),
        cost_estimate=pl.CostEstimate(flops=1 << 20, bytes_accessed=1 << 20, transcendentals=0),
        name="row_weights",
    )(scale, parts)
    weights = lax.all_to_all(copies, SEQ, split_axis=0, concat_axis=0, tiled=True)
    weights = weights.reshape(H * positions, positions)

    part_rows = tokens // CHUNKS
    mixed = call(
        mix_kernel,
        meta,
        (weights, rv, flat),
        (steps,),
        [whole_spec((H * positions, positions)), row_spec(step_rows, width), row_spec(step_rows, width)],
        [row_spec(step_rows, width)] + [whole_spec((part_rows, width))] * CHUNKS,
        [jax.ShapeDtypeStruct((tokens, width), BF16)]
        + [jax.ShapeDtypeStruct((part_rows, width), BF16)] * CHUNKS,
        [pltpu.VMEM((sequences, positions, width), F32)],
        pl.CostEstimate(flops=4 * tokens * width * positions, bytes_accessed=8 << 20, transcendentals=0),
        "row_mix",
    )
    row_out, sends = mixed[0], mixed[1:]

    columns = positions // groups // CHUNKS
    lanes = 2 * LANES
    each = positions // CHUNKS
    returned = []
    arrived = [
        lax.all_to_all(
            s.reshape(groups, part_rows // groups, width), SEQ, split_axis=0, concat_axis=0, tiled=True
        )
        for s in sends
    ]
    for got in arrived:
        out = call(
            functools.partial(column_kernel, columns),
            meta,
            (got.reshape(part_rows, width), vq, vk, vv),
            (width // lanes,),
            [whole_spec((part_rows, width))]
            + [pl.BlockSpec((width, lanes), lambda i, *_: (0, i))] * 3,
            pl.BlockSpec((part_rows, lanes), lambda i, *_: (0, i)),
            jax.ShapeDtypeStruct((part_rows, width), BF16),
            [],
            pl.CostEstimate(
                flops=6 * part_rows * width * width, bytes_accessed=6 << 20, transcendentals=0
            ),
            "columns",
        )
        returned.append(
            lax.all_to_all(
                out.reshape(groups, part_rows // groups, width),
                SEQ,
                split_axis=0,
                concat_axis=0,
                tiled=True,
            )
        )
    result = None
    block = 16
    count_blocks = each // block
    for k, got in enumerate(returned):
        args = [got.reshape(part_rows, width)]
        in_specs = [pl.BlockSpec((block * sequences, width), lambda i: (i, 0))]
        if k > 0:
            args.append(result)
            in_specs.append(pl.BlockSpec(memory_space=pl.ANY))
        result = pl.pallas_call(
            turn_kernel if k == 0 else turn_into,
            grid=(count_blocks,),
            in_specs=in_specs,
            out_specs=pl.BlockSpec(
                (sequences, block, width), lambda i, k=k: (0, k * count_blocks + i, 0)
            ),
            out_shape=jax.ShapeDtypeStruct((sequences, positions, width), BF16),
            input_output_aliases={} if k == 0 else {1: 0},
            cost_estimate=pl.CostEstimate(flops=0, bytes_accessed=3 << 20, transcendentals=0),
            name="turn_back",
        )(*args)
    return row_out.reshape(sequences, positions, width), result


def solution(mesh):
    whole = P(("aln", "seq"), None, None)
    in_specs = (whole, P("aln"), P(), P(), P(), P(), P(), P())
    return jax.shard_map(
        local, mesh=mesh, in_specs=in_specs, out_specs=(whole, whole), check_vma=False
    )
```

time: 232 us -> 178 us (0.77)
  the two profiles are of different devices: /device:TPU:4 before, /device:TPU:2 now
where the time goes in v1:
time: 178 us; the launch traced here: 177 us
  waiting for transfers between devices  68.9 us (39%)
  Pallas kernels  44.4 us (25%)
  starting transfers between devices  30.4 us (17%)
  blocking collectives  26.4 us (15%)
  matrix products  2.53 us (1%)
  local copies, waits for them, and re-layouts  2.42 us (1%)
    pallas_call x4, Pallas kernels, call(): pl.pallas_call(kernel, grid_spec=pltpu.PrefetchScalarGridSpec(num_scalar_...  35.5 us
    all_to_all x2, waiting for transfers between devices, local(): lax.all_to_all(out.reshape(groups, part_rows // groups, width), SEQ, spli...  29.8 us
    all_to_all x1, blocking collectives, local(): lax.all_to_all(s.reshape(groups, part_rows // groups, width), SEQ, split_...  26.4 us
    all_to_all x1, waiting for transfers between devices, local(): lax.all_to_all(logits.reshape(groups, share, positions), SEQ, split_axis=...  15.2 us
    all_to_all x1, waiting for transfers between devices, local(): lax.all_to_all(copies, SEQ, split_axis=0, concat_axis=0, tiled=True)  12.1 us
    all_to_all x1, waiting for transfers between devices, local(): lax.all_to_all(s.reshape(groups, part_rows // groups, width), SEQ, split_...  11.8 us
    all_to_all x1, starting transfers between devices, local(): lax.all_to_all(logits.reshape(groups, share, positions), SEQ, split_axis=...  11.6 us
    all_to_all x2, starting transfers between devices, local(): lax.all_to_all(out.reshape(groups, part_rows // groups, width), SEQ, spli...  9.62 us
  transfers between devices with their start and end apart: 5, of which 5 were waited for; matrix products, arithmetic and copies ran while one was open for 1% of the time, Pallas kernels for 13%

profile of v1, /device:TPU:2, one launch (start us, length us, event | category | flops | bytes accessed | tf_op | source)
XLA Modules:
  0.0 177.2 jit_solution(626021293855267726)
XLA Ops:
  0.6 0.0 copy-start
  1.4 0.6 pad_add_fusion.meta
  2.0 9.0 %row_logits.1 = (bf16[1024,768]{1,0:T(8,128)(2,1)}, bf16[1536,128]{1,0:T(8,128)(2,1)}) custom-call(s32[2]{0:T(128)} %pad_add_fusion.meta, bf16[1024,768]{1,0:T(8,128)(2,1)} %bitcast.17, bf16[768,768]{1,0:T(8,128)(2,1)} %wq_ref.3, bf16[768,768]{1,0:T(8,128)(2,1)} %wk_ref.3), custom_call_target="tpu_custom_call" | custom-call | flops 2415919104 | bytes 6291456 | tf_op jit(solution)/shard_map/row_logits/pallas_call | solution.py:196
  11.0 11.6 %all-to-all-start = ((bf16[32,48,128]{2,1,0:T(8,128)(2,1)}), bf16[32,48,128]{2,1,0:T(8,128)(2,1)S(1)}, u32[]{:S(2)}, u32[]{:S(2)}) async-start(bf16[32,48,128]{2,1,0:T(8,128)(2,1)} %bitcast.25), calls=%async_computation | async-start | bytes 786432 | tf_op jit(solution)/shard_map/all_to_all | solution.py:241
  22.7 15.2 %all-to-all-done.parts_ref = bf16[32,48,128]{2,1,0:T(8,128)(2,1)S(1)} async-done(((bf16[32,48,128]{2,1,0:T(8,128)(2,1)}), bf16[32,48,128]{2,1,0:T(8,128)(2,1)S(1)}, u32[]{:S(2)}, u32[]{:S(2)}) %all-to-all-start) | async-done | bytes 393248 | tf_op jit(solution)/shard_map/all_to_all | solution.py:241
  38.0 0.7 copy-done.3
  38.7 2.0 %row_weights.1 = bf16[32,48,128]{2,1,0:T(8,128)(2,1)} custom-call(f32[1]{0:T(128)S(6)} %div.4.scale_ref, bf16[32,48,128]{2,1,0:T(8,128)(2,1)} %copy-done.3), custom_call_target="tpu_custom_call" | custom-call | flops 1048576 | bytes 1048576 | tf_op jit(solution)/shard_map/row_weights/pallas_call | solution.py:246
  40.7 4.3 %all-to-all-start.1 = ((bf16[32,48,128]{2,1,0:T(8,128)(2,1)}), bf16[32,48,128]{2,1,0:T(8,128)(2,1)S(1)}, u32[]{:S(2)}, u32[]{:S(2)}) async-start(bf16[32,48,128]{2,1,0:T(8,128)(2,1)} %row_weights.1), calls=%async_computation.1 | async-start | bytes 786432 | tf_op jit(solution)/shard_map/all_to_all | solution.py:257
  45.0 2.5 %convolution_convert_fusion.rv_ref = bf16[1024,768]{1,0:T(8,128)(2,1)} fusion(bf16[1024,768]{1,0:T(8,128)(2,1)S(1)} %copy-done.6, bf16[768,768]{1,0:T(8,128)(2,1)S(1)} %copy-done), kind=kOutput, calls=%fused_computation | convolution fusion | flops 1208745984 | bytes 4325376 | tf_op jit(solution)/shard_map/dot_general | solution.py:244
  47.5 12.1 %all-to-all-done.1 = bf16[32,48,128]{2,1,0:T(8,128)(2,1)S(1)} async-done(((bf16[32,48,128]{2,1,0:T(8,128)(2,1)}), bf16[32,48,128]{2,1,0:T(8,128)(2,1)S(1)}, u32[]{:S(2)}, u32[]{:S(2)}) %all-to-all-start.1) | async-done | bytes 393248 | tf_op jit(solution)/shard_map/all_to_all | solution.py:257
  59.7 0.8 copy-done.4
  60.5 6.8 %row_mix.1 = (bf16[1024,768]{1,0:T(8,128)(2,1)}, bf16[512,768]{1,0:T(8,128)(2,1)}, bf16[512,768]{1,0:T(8,128)(2,1)}) custom-call(s32[2]{0:T(128)} %pad_add_fusion.meta, bf16[1536,128]{1,0:T(8,128)(2,1)} %bitcast.19, bf16[1024,768]{1,0:T(8,128)(2,1)} %convolution_convert_fusion.rv_ref, bf16[1024,768]{1,0:T(8,128)(2,1)} %bitcast.18), custom_call_target="tpu_custom_call" | custom-call | flops 402653184 | bytes 8388608 | tf_op jit(solution)/shard_map/row_mix/pallas_call | solution.py:196
  67.2 26.4 %all_to_all.30 = bf16[32,16,768]{2,1,0:T(8,128)(2,1)} all-to-all(bf16[32,16,768]{2,1,0:T(8,128)(2,1)} %bitcast.24), channel_id=1, replica_groups=mesh['aln'=8,'seq'=32] {'seq'}, dimensions={0} | all-to-all | bytes 1572864 | tf_op jit(solution)/shard_map/all_to_all | solution.py:281
  93.7 4.8 %all-to-all-start.2 = ((bf16[32,16,768]{2,1,0:T(8,128)(2,1)}), bf16[32,16,768]{2,1,0:T(8,128)(2,1)S(1)}, u32[]{:S(2)}, u32[]{:S(2)}) async-start(bf16[32,16,768]{2,1,0:T(8,128)(2,1)} %bitcast.5), calls=%async_computation.2 | async-start | bytes 1572864 | tf_op jit(solution)/shard_map/all_to_all | solution.py:281
  98.5 9.9 %columns.3 = bf16[512,768]{1,0:T(8,128)(2,1)} custom-call(s32[2]{0:T(128)} %pad_add_fusion.meta, bf16[512,768]{1,0:T(8,128)(2,1)} %bitcast.23, bf16[768,768]{1,0:T(8,128)(2,1)} %wq_ref.5, bf16[768,768]{1,0:T(8,128)(2,1)} %wk_ref.5, bf16[768,768]{1,0:T(8,128)(2,1)} %wv_ref.3), custom_call_target="tpu_custom_call" | custom-call | flops 1811939328 | bytes 6291456 | tf_op jit(solution)/shard_map/columns/pallas_call | solution.py:196
  108.4 11.8 %all-to-all-done.2 = bf16[32,16,768]{2,1,0:T(8,128)(2,1)S(1)} async-done(((bf16[32,16,768]{2,1,0:T(8,128)(2,1)}), bf16[32,16,768]{2,1,0:T(8,128)(2,1)S(1)}, u32[]{:S(2)}, u32[]{:S(2)}) %all-to-all-start.2) | async-done | bytes 786464 | tf_op jit(solution)/shard_map/all_to_all | solution.py:281
  120.2 4.8 %all-to-all-start.5 = ((bf16[32,16,768]{2,1,0:T(8,128)(2,1)}), bf16[32,16,768]{2,1,0:T(8,128)(2,1)S(1)}, u32[]{:S(2)}, u32[]{:S(2)}) async-start(bf16[32,16,768]{2,1,0:T(8,128)(2,1)} %bitcast.21), calls=%async_computation.5 | async-start | bytes 1572864 | tf_op jit(solution)/shard_map/all_to_all | solution.py:303
  125.0 9.9 %columns.2 = bf16[512,768]{1,0:T(8,128)(2,1)} custom-call(s32[2]{0:T(128)} %pad_add_fusion.meta, bf16[512,768]{1,0:T(8,128)(2,1)} %bitcast.20, bf16[768,768]{1,0:T(8,128)(2,1)} %wq_ref.5, bf16[768,768]{1,0:T(8,128)(2,1)} %wk_ref.5, bf16[768,768]{1,0:T(8,128)(2,1)} %wv_ref.3), custom_call_target="tpu_custom_call" | custom-call | flops 1811939328 | bytes 6291456 | tf_op jit(solution)/shard_map/columns/pallas_call | solution.py:196
  134.8 11.7 %all-to-all-done.5 = bf16[32,16,768]{2,1,0:T(8,128)(2,1)S(1)} async-done(((bf16[32,16,768]{2,1,0:T(8,128)(2,1)}), bf16[32,16,768]{2,1,0:T(8,128)(2,1)S(1)}, u32[]{:S(2)}, u32[]{:S(2)}) %all-to-all-start.5) | async-done | bytes 786464 | tf_op jit(solution)/shard_map/all_to_all | solution.py:303
  146.5 4.8 %all-to-all-start.3 = ((bf16[32,16,768]{2,1,0:T(8,128)(2,1)}), bf16[32,16,768]{2,1,0:T(8,128)(2,1)S(1)}, u32[]{:S(2)}, u32[]{:S(2)}) async-start(bf16[32,16,768]{2,1,0:T(8,128)(2,1)} %bitcast.22), calls=%async_computation.3 | async-start | bytes 1572864 | tf_op jit(solution)/shard_map/all_to_all | solution.py:303
  151.4 3.4 %turn_back.2.kept_ref = bf16[8,128,768]{2,1,0:T(8,128)(2,1)} custom-call(bf16[512,768]{1,0:T(8,128)(2,1)} %bitcast.15), custom_call_target="tpu_custom_call" | custom-call | bytes 3145728 | tf_op jit(solution)/shard_map/turn_back/pallas_call | solution.py:320
  154.8 18.1 %all-to-all-done.3 = bf16[32,16,768]{2,1,0:T(8,128)(2,1)S(1)} async-done(((bf16[32,16,768]{2,1,0:T(8,128)(2,1)}), bf16[32,16,768]{2,1,0:T(8,128)(2,1)S(1)}, u32[]{:S(2)}, u32[]{:S(2)}) %all-to-all-start.3) | async-done | bytes 786464 | tf_op jit(solution)/shard_map/all_to_all | solution.py:303
  172.9 0.9 copy-done.2
  173.8 3.4 %turn_back.3 = bf16[8,128,768]{2,1,0:T(8,128)(2,1)} custom-call(bf16[512,768]{1,0:T(8,128)(2,1)} %bitcast.16, bf16[8,128,768]{2,1,0:T(8,128)(2,1)} %turn_back.2.kept_ref), custom_call_target="tpu_custom_call", output_to_operand_aliasing={{}: (1, {})} | custom-call | bytes 3145728 | tf_op jit(solution)/shard_map/turn_back/pallas_call | solution.py:320
  (10 shorter events, 0.0 us)
Async XLA Ops:
  0.6 44.4 %copy-start = (bf16[768,768]{1,0:T(8,128)(2,1)S(1)}, bf16[768,768]{1,0:T(8,128)(2,1)}, u32[]{:S(2)}) copy-start(bf16[768,768]{1,0:T(8,128)(2,1)} %param.12) | copy-start | bytes 3538948
  11.0 34.0 %copy-start.6 = (bf16[1024,768]{1,0:T(8,128)(2,1)S(1)}, bf16[1024,768]{1,0:T(8,128)(2,1)}, u32[]{:S(2)}) copy-start(bf16[1024,768]{1,0:T(8,128)(2,1)} %get-tuple-element.8) | copy-start | bytes 4718596
  11.0 26.9 %all-to-all-start = ((bf16[32,48,128]{2,1,0:T(8,128)(2,1)}), bf16[32,48,128]{2,1,0:T(8,128)(2,1)S(1)}, u32[]{:S(2)}, u32[]{:S(2)}) async-start(bf16[32,48,128]{2,1,0:T(8,128)(2,1)} %bitcast.25), calls=%async_computation | async-start | bytes 786432 | tf_op jit(solution)/shard_map/all_to_all | solution.py:241
  38.0 0.7 copy-start.3
  40.7 19.0 %all-to-all-start.1 = ((bf16[32,48,128]{2,1,0:T(8,128)(2,1)}), bf16[32,48,128]{2,1,0:T(8,128)(2,1)S(1)}, u32[]{:S(2)}, u32[]{:S(2)}) async-start(bf16[32,48,128]{2,1,0:T(8,128)(2,1)} %row_weights.1), calls=%async_computation.1 | async-start | bytes 786432 | tf_op jit(solution)/shard_map/all_to_all | solution.py:257
  59.7 0.8 copy-start.4
  93.7 26.5 %all-to-all-start.2 = ((bf16[32,16,768]{2,1,0:T(8,128)(2,1)}), bf16[32,16,768]{2,1,0:T(8,128)(2,1)S(1)}, u32[]{:S(2)}, u32[]{:S(2)}) async-start(bf16[32,16,768]{2,1,0:T(8,128)(2,1)} %bitcast.5), calls=%async_computation.2 | async-start | bytes 1572864 | tf_op jit(solution)/shard_map/all_to_all | solution.py:281
  120.2 4.8 %copy-start.5 = (bf16[32,16,768]{2,1,0:T(8,128)(2,1)}, bf16[32,16,768]{2,1,0:T(8,128)(2,1)S(1)}, u32[]{:S(2)}) copy-start(bf16[32,16,768]{2,1,0:T(8,128)(2,1)S(1)} %all-to-all-done.2) | copy-start | bytes 2359300
  120.2 26.4 %all-to-all-start.5 = ((bf16[32,16,768]{2,1,0:T(8,128)(2,1)}), bf16[32,16,768]{2,1,0:T(8,128)(2,1)S(1)}, u32[]{:S(2)}, u32[]{:S(2)}) async-start(bf16[32,16,768]{2,1,0:T(8,128)(2,1)} %bitcast.21), calls=%async_computation.5 | async-start | bytes 1572864 | tf_op jit(solution)/shard_map/all_to_all | solution.py:303
  146.5 4.8 %copy-start.1 = (bf16[32,16,768]{2,1,0:T(8,128)(2,1)}, bf16[32,16,768]{2,1,0:T(8,128)(2,1)S(1)}, u32[]{:S(2)}) copy-start(bf16[32,16,768]{2,1,0:T(8,128)(2,1)S(1)} %all-to-all-done.5) | copy-start | bytes 2359300
  146.5 26.3 %all-to-all-start.3 = ((bf16[32,16,768]{2,1,0:T(8,128)(2,1)}), bf16[32,16,768]{2,1,0:T(8,128)(2,1)S(1)}, u32[]{:S(2)}, u32[]{:S(2)}) async-start(bf16[32,16,768]{2,1,0:T(8,128)(2,1)} %bitcast.22), calls=%async_computation.3 | async-start | bytes 1572864 | tf_op jit(solution)/shard_map/all_to_all | solution.py:303
  172.9 0.9 copy-start.2

commit v2 on v1

--- a/solution.py
+++ b/solution.py
@@ -35,17 +35,22 @@
     return value[:, index * LANES : (index + 1) * LANES]
 
 
-def logits_kernel(meta, x_ref, wq_ref, wk_ref, normed_ref, logits_ref, total):
+def logits_kernel(tally, x_ref, wq_ref, wk_ref, wv_ref, rv_ref, logits_ref, total):
     step = pl.program_id(0)
     rows = x_ref.shape[0] // 2
-    first, count = meta[0], meta[1]
+    first, count = lax.axis_index(SEQ) * (2 * pl.num_programs(0)), tally[0]
+
+    @pl.when((step == 0) & (lax.rem(lax.axis_index("aln"), 2) == 1))
+    def _():
+        pl.delay(STAGGER)
+
     normed = standardize(x_ref[...].astype(F32)).astype(BF16)
-    normed_ref[...] = normed
     row = lax.broadcasted_iota(jnp.int32, (2 * rows, 1), 0)
     sequence = first + 2 * step + (row >= rows).astype(jnp.int32)
     live = (sequence < count).astype(F32)
     q = (jnp.dot(normed, wq_ref[...], preferred_element_type=F32) * live).astype(BF16)
     k = jnp.dot(normed, wk_ref[...], preferred_element_type=F32).astype(BF16)
+    rv_ref[...] = jnp.dot(normed, wv_ref[...], preferred_element_type=F32).astype(BF16)
     low, high = half_masks()
 
     @pl.when(step == 0)
@@ -68,11 +73,12 @@
         logits_ref[...] = total[...].astype(BF16)
 
 
-def weights_kernel(scale_ref, parts_ref, out_ref):
+def weights_kernel(tally, parts_ref, out_ref):
     logits = parts_ref[0].astype(F32)
     for source in range(1, parts_ref.shape[0]):
         logits += parts_ref[source].astype(F32)
-    logits = logits * scale_ref[0]
+    count = jnp.full((1, 1), tally[0], jnp.int32).astype(F32)
+    logits = logits / (jnp.sqrt(F32(DH)) * jnp.sqrt(count))
     top = jnp.max(logits, axis=-1, keepdims=True)
     powers = jnp.exp(logits - top)
     weights = (powers / jnp.sum(powers, axis=-1, keepdims=True)).astype(BF16)
@@ -80,11 +86,11 @@
         out_ref[target] = weights
 
 
-def mix_kernel(meta, w_ref, rv_ref, x_ref, row_ref, *rest):
+def mix_kernel(tally, w_ref, rv_ref, x_ref, row_ref, *rest):
     sends, held = rest[:-1], rest[-1]
     step = pl.program_id(0)
     rows = x_ref.shape[0] // 2
-    first, count = meta[0], meta[1]
+    first, count = lax.axis_index(SEQ) * held.shape[0], tally[0]
     low, high = half_masks()
     mixed = [[], []]
     for pair in range(H // 2):
@@ -119,8 +125,8 @@
                 send[block * span : (block + 1) * span, :] = flat.astype(BF16)
 
 
-def column_kernel(columns, meta, n_ref, wq_ref, wk_ref, wv_ref, out_ref):
-    count = meta[1]
+def column_kernel(columns, tally, n_ref, wq_ref, wk_ref, wv_ref, out_ref):
+    count = tally[0]
     rows = n_ref.shape[0]
     total = rows // columns
     width = wq_ref.shape[1]
@@ -174,16 +180,6 @@
     out_ref[...] = stacked.reshape(rows, width).astype(BF16)
 
 
-def turn_kernel(recv_ref, out_ref):
-    sequences, size = out_ref.shape[0], out_ref.shape[1]
-    got = recv_ref[...].astype(F32).reshape(size, sequences, recv_ref.shape[1])
-    out_ref[...] = jnp.swapaxes(got, 0, 1).astype(BF16)
-
-
-def turn_into(recv_ref, kept_ref, out_ref):
-    turn_kernel(recv_ref, out_ref)
-
-
 def row_spec(rows, width):
     return pl.BlockSpec((rows, width), lambda i, *_: (i, 0))
 
@@ -192,7 +188,7 @@
     return pl.BlockSpec(shape, lambda i, *_: (0,) * len(shape))
 
 
-def call(kernel, meta, args, grid, in_specs, out_specs, out_shape, scratch, cost, name):
+def call(kernel, meta, args, grid, in_specs, out_specs, out_shape, scratch, cost, name, vmem):
     return pl.pallas_call(
         kernel,
         grid_spec=pltpu.PrefetchScalarGridSpec(
@@ -204,45 +200,50 @@
         ),
         out_shape=out_shape,
         cost_estimate=cost,
-        compiler_params=pltpu.CompilerParams(dimension_semantics=("arbitrary",) * len(grid)),
+        compiler_params=pltpu.CompilerParams(
+            dimension_semantics=("arbitrary",) * len(grid), vmem_limit_bytes=vmem << 20
+        ),
         name=name,
     )(meta, *args)
 
 
-CHUNKS = 2
+STAGGER = 22000
+
+
+def exchange(value):
+    return lax.all_to_all(value, SEQ, split_axis=0, concat_axis=0, tiled=True)
+
+
+def in_hbm(*arrays):
+    return tuple(pltpu.with_memory_space_constraint(a, pltpu.HBM) for a in arrays)
 
 
 def local(x, tallies, hq, hk, hv, vq, vk, vv):
     sequences, positions, width = x.shape
     groups = lax.axis_size(SEQ)
     tokens = sequences * positions
-    count = tallies[0]
-    meta = jnp.stack([lax.axis_index(SEQ) * sequences, count]).astype(jnp.int32)
     flat = x.reshape(tokens, width)
     step_rows = 2 * positions
     steps = tokens // step_rows
     share = H * positions // groups
 
-    normed, logits = call(
+    rv, logits = call(
         logits_kernel,
-        meta,
-        (flat, hq, hk),
+        tallies,
+        in_hbm(flat, hq, hk, hv),
         (steps,),
-        [row_spec(step_rows, width), whole_spec((width, width)), whole_spec((width, width))],
+        [row_spec(step_rows, width)] + [whole_spec((width, width))] * 3,
         [row_spec(step_rows, width), whole_spec((H * positions, positions))],
         [
             jax.ShapeDtypeStruct((tokens, width), BF16),
             jax.ShapeDtypeStruct((H * positions, positions), BF16),
         ],
         [pltpu.VMEM((H * positions, positions), F32)],
-        pl.CostEstimate(flops=4 * tokens * width * width, bytes_accessed=6 << 20, transcendentals=0),
+        pl.CostEstimate(flops=6 * tokens * width * width, bytes_accessed=6 << 20, transcendentals=0),
         "row_logits",
+        24,
     )
-    parts = lax.all_to_all(
-        logits.reshape(groups, share, positions), SEQ, split_axis=0, concat_axis=0, tiled=True
-    )
-    rv = jnp.dot(normed, hv, preferred_element_type=F32).astype(BF16)
-    scale = (1.0 / (jnp.sqrt(F32(DH)) * jnp.sqrt(count.astype(F32)))).reshape(1)
+    parts = exchange(logits.reshape(groups, share, positions))
     copies = pl.pallas_call(
         weights_kernel,
         in_specs=[
@@ -252,83 +253,42 @@
         out_specs=pl.BlockSpec(memory_space=pltpu.VMEM),
         out_shape=jax.ShapeDtypeStruct((groups, share, positions), BF16),
         cost_estimate=pl.CostEstimate(flops=1 << 20, bytes_accessed=1 << 20, transcendentals=0),
+        compiler_params=pltpu.CompilerParams(vmem_limit_bytes=8 << 20),
         name="row_weights",
-    )(scale, parts)
-    weights = lax.all_to_all(copies, SEQ, split_axis=0, concat_axis=0, tiled=True)
-    weights = weights.reshape(H * positions, positions)
-
-    part_rows = tokens // CHUNKS
-    mixed = call(
+    )(tallies, parts)
+    weights = exchange(copies).reshape(H * positions, positions)
+    rv, flat = in_hbm(rv, flat)
+    row_out, send = call(
         mix_kernel,
-        meta,
+        tallies,
         (weights, rv, flat),
         (steps,),
         [whole_spec((H * positions, positions)), row_spec(step_rows, width), row_spec(step_rows, width)],
-        [row_spec(step_rows, width)] + [whole_spec((part_rows, width))] * CHUNKS,
-        [jax.ShapeDtypeStruct((tokens, width), BF16)]
-        + [jax.ShapeDtypeStruct((part_rows, width), BF16)] * CHUNKS,
+        [row_spec(step_rows, width), whole_spec((tokens, width))],
+        [jax.ShapeDtypeStruct((tokens, width), BF16)] * 2,
         [pltpu.VMEM((sequences, positions, width), F32)],
         pl.CostEstimate(flops=4 * tokens * width * positions, bytes_accessed=8 << 20, transcendentals=0),
         "row_mix",
+        24,
     )
-    row_out, sends = mixed[0], mixed[1:]
-
-    columns = positions // groups // CHUNKS
+    columns = positions // groups
     lanes = 2 * LANES
-    each = positions // CHUNKS
-    returned = []
-    arrived = [
-        lax.all_to_all(
-            s.reshape(groups, part_rows // groups, width), SEQ, split_axis=0, concat_axis=0, tiled=True
-        )
-        for s in sends
-    ]
-    for got in arrived:
-        out = call(
-            functools.partial(column_kernel, columns),
-            meta,
-            (got.reshape(part_rows, width), vq, vk, vv),
-            (width // lanes,),
-            [whole_spec((part_rows, width))]
-            + [pl.BlockSpec((width, lanes), lambda i, *_: (0, i))] * 3,
-            pl.BlockSpec((part_rows, lanes), lambda i, *_: (0, i)),
-            jax.ShapeDtypeStruct((part_rows, width), BF16),
-            [],
-            pl.CostEstimate(
-                flops=6 * part_rows * width * width, bytes_accessed=6 << 20, transcendentals=0
-            ),
-            "columns",
-        )
-        returned.append(
-            lax.all_to_all(
-                out.reshape(groups, part_rows // groups, width),
-                SEQ,
-                split_axis=0,
-                concat_axis=0,
-                tiled=True,
-            )
-        )
-    result = None
-    block = 16
-    count_blocks = each // block
-    for k, got in enumerate(returned):
-        args = [got.reshape(part_rows, width)]
-        in_specs = [pl.BlockSpec((block * sequences, width), lambda i: (i, 0))]
-        if k > 0:
-            args.append(result)
-            in_specs.append(pl.BlockSpec(memory_space=pl.ANY))
-        result = pl.pallas_call(
-            turn_kernel if k == 0 else turn_into,
-            grid=(count_blocks,),
-            in_specs=in_specs,
-            out_specs=pl.BlockSpec(
-                (sequences, block, width), lambda i, k=k: (0, k * count_blocks + i, 0)
-            ),
-            out_shape=jax.ShapeDtypeStruct((sequences, positions, width), BF16),
-            input_output_aliases={} if k == 0 else {1: 0},
-            cost_estimate=pl.CostEstimate(flops=0, bytes_accessed=3 << 20, transcendentals=0),
-            name="turn_back",
-        )(*args)
+    got = exchange(send.reshape(groups, tokens // groups, width)).reshape(tokens, width)
+    out = call(
+        functools.partial(column_kernel, columns),
+        tallies,
+        (got, vq, vk, vv),
+        (width // lanes,),
+        [whole_spec((tokens, width))] + [pl.BlockSpec((width, lanes), lambda i, *_: (0, i))] * 3,
+        pl.BlockSpec((tokens, lanes), lambda i, *_: (0, i)),
+        jax.ShapeDtypeStruct((tokens, width), BF16),
+        [],
+        pl.CostEstimate(flops=6 * tokens * width * width, bytes_accessed=6 << 20, transcendentals=0),
+        "columns",
+        40,
+    )
+    back = exchange(out.reshape(groups, tokens // groups, width))
+    result = jnp.swapaxes(back.reshape(positions, sequences, width), 0, 1)
     return row_out.reshape(sequences, positions, width), result
 
 

time: 178 us -> 150 us (0.84)
  the two profiles are of different devices: /device:TPU:2 before, /device:TPU:1 now
where the time goes in v2:
time: 150 us
  blocking collectives  96.4 us (64%)
  Pallas kernels  50.5 us (34%)
    all_to_all x4, blocking collectives, exchange(): return lax.all_to_all(value, SEQ, split_axis=0, concat_axis=0, tiled=True)  96.4 us
    pallas_call x3, Pallas kernels, call(): pl.pallas_call(kernel, grid_spec=pltpu.PrefetchScalarGridSpec(num_scalar_...  50.2 us

profile of v2, /device:TPU:1, one launch (start us, length us, event | category | flops | bytes accessed | tf_op | source)
XLA Modules:
  0.0 149.7 jit_solution(1530673123415973466)
XLA Ops:
  1.3 31.6 %row_logits.1 = (bf16[1024,768]{1,0:T(8,128)(2,1)S(1)}, bf16[1536,128]{1,0:T(8,128)(2,1)S(1)}) custom-call(s32[1]{0:T(128)S(6)} %copy.11.tally, bf16[1024,768]{1,0:T(8,128)(2,1)} %bitcast.16, bf16[768,768]{1,0:T(8,128)(2,1)} %wq_ref.2, bf16[768,768]{1,0:T(8,128)(2,1)} %wk_ref.2, bf16[768,768]{1,0:T(8,128)(2,1)} %wv_ref.2), custom_call_target="tpu_custom_call" | custom-call | flops 3623878656 | bytes 6291456 | tf_op jit(solution)/shard_map/row_logits/pallas_call | solution.py:192
  32.9 0.0 copy-start
  32.9 24.1 %all_to_all.20.parts_ref = bf16[32,48,128]{2,1,0:T(8,128)(2,1)S(1)} all-to-all(bf16[32,48,128]{2,1,0:T(8,128)(2,1)S(1)} %bitcast.14), channel_id=1, replica_groups=mesh['aln'=8,'seq'=32] {'seq'}, dimensions={0} | all-to-all | bytes 786432 | tf_op jit(solution)/shard_map/all_to_all | solution.py:214
  57.0 0.2 row_weights.1
  57.3 14.8 %all_to_all.21 = bf16[32,48,128]{2,1,0:T(8,128)(2,1)S(1)} all-to-all(bf16[32,48,128]{2,1,0:T(8,128)(2,1)S(1)} %row_weights.1), channel_id=1, replica_groups=mesh['aln'=8,'seq'=32] {'seq'}, dimensions={0} | all-to-all | bytes 786432 | tf_op jit(solution)/shard_map/all_to_all | solution.py:214
  72.0 0.0 copy-done
  72.0 0.0 copy-start.3
  72.0 5.5 %row_mix.1 = (bf16[1024,768]{1,0:T(8,128)(2,1)}, bf16[1024,768]{1,0:T(8,128)(2,1)S(1)}) custom-call(s32[1]{0:T(128)S(6)} %copy.11.tally, bf16[1536,128]{1,0:T(8,128)(2,1)S(1)} %bitcast.13, bf16[1024,768]{1,0:T(8,128)(2,1)} %copy-done, bf16[1024,768]{1,0:T(8,128)(2,1)} %bitcast.17), custom_call_target="tpu_custom_call" | custom-call | flops 402653184 | bytes 8388608 | tf_op jit(solution)/shard_map/row_mix/pallas_call | solution.py:192
  77.6 0.0 copy-start.1
  77.6 0.0 copy-start.2
  77.6 29.5 %all_to_all.22 = bf16[32,32,768]{2,1,0:T(8,128)(2,1)S(1)} all-to-all(bf16[32,32,768]{2,1,0:T(8,128)(2,1)S(1)} %bitcast.10), channel_id=1, replica_groups=mesh['aln'=8,'seq'=32] {'seq'}, dimensions={0} | all-to-all | bytes 3145728 | tf_op jit(solution)/shard_map/all_to_all | solution.py:214
  107.1 0.0 copy-done.3
  107.1 0.0 copy-done.1
  107.1 0.0 copy-done.2
  107.1 13.1 %columns.1 = bf16[1024,768]{1,0:T(8,128)(2,1)S(1)} custom-call(s32[1]{0:T(128)S(6)} %copy.11.tally, bf16[1024,768]{1,0:T(8,128)(2,1)S(1)} %bitcast.11, bf16[768,768]{1,0:T(8,128)(2,1)S(1)} %copy-done.1, bf16[768,768]{1,0:T(8,128)(2,1)S(1)} %copy-done.2, bf16[768,768]{1,0:T(8,128)(2,1)S(1)} %copy-done.3), custom_call_target="tpu_custom_call" | custom-call | flops 3623878656 | bytes 6291456 | tf_op jit(solution)/shard_map/columns/pallas_call | solution.py:192
  120.3 28.0 %all_to_all.23 = bf16[32,32,768]{2,1,0:T(8,128)(2,1)S(1)} all-to-all(bf16[32,32,768]{2,1,0:T(8,128)(2,1)S(1)} %bitcast.12), channel_id=1, replica_groups=mesh['aln'=8,'seq'=32] {'seq'}, dimensions={0} | all-to-all | bytes 3145728 | tf_op jit(solution)/shard_map/all_to_all | solution.py:214
  148.2 1.4 copy.10
Async XLA Ops:
  32.9 39.2 %copy-start = (bf16[1024,768]{1,0:T(8,128)(2,1)}, bf16[1024,768]{1,0:T(8,128)(2,1)S(1)}, u32[]{:S(2)}) copy-start(bf16[1024,768]{1,0:T(8,128)(2,1)S(1)} %get-tuple-element.7.rv_ref) | copy-start | bytes 4718596
  72.0 35.1 %copy-start.3 = (bf16[768,768]{1,0:T(8,128)(2,1)S(1)}, bf16[768,768]{1,0:T(8,128)(2,1)}, u32[]{:S(2)}) copy-start(bf16[768,768]{1,0:T(8,128)(2,1)} %wv_ref.3) | copy-start | bytes 3538948
  77.6 29.5 %copy-start.1 = (bf16[768,768]{1,0:T(8,128)(2,1)S(1)}, bf16[768,768]{1,0:T(8,128)(2,1)}, u32[]{:S(2)}) copy-start(bf16[768,768]{1,0:T(8,128)(2,1)} %wq_ref.3) | copy-start | bytes 3538948
  77.6 29.5 %copy-start.2 = (bf16[768,768]{1,0:T(8,128)(2,1)S(1)}, bf16[768,768]{1,0:T(8,128)(2,1)}, u32[]{:S(2)}) copy-start(bf16[768,768]{1,0:T(8,128)(2,1)} %wk_ref.3) | copy-start | bytes 3538948

commit v3 on v2

v3 whole, which is shorter than its diff:
```python
import math

import jax
import jax.numpy as jnp
from jax import lax
from jax.experimental import pallas as pl
from jax.experimental.pallas import tpu as pltpu
from jax.sharding import PartitionSpec as P

H = 12
DH = 64
SEQ = "seq"
LANES = 128
EPS = 1e-05
BF16 = jnp.bfloat16
F32 = jnp.float32
NT = (((1,), (1,)), ((), ()))


def standardize(values):
    centre = jnp.mean(values, axis=-1, keepdims=True)
    shifted = values - centre
    spread = jnp.mean(shifted * shifted, axis=-1, keepdims=True)
    return shifted * lax.rsqrt(spread + EPS)


def half_masks():
    lane = lax.broadcasted_iota(jnp.int32, (1, LANES), 1)
    low = (lane < DH).astype(F32)
    return low.astype(BF16), (1.0 - low).astype(BF16)


def lane_block(value, index):
    return value[:, index * LANES : (index + 1) * LANES]


def fetch(refs, sems):
    copies = [pltpu.make_async_copy(src, dst, sems.at[i]) for i, (src, dst) in enumerate(refs)]
    for copy in copies:
        copy.start()
    return copies


def logits_kernel(
    tally, x_hbm, wq_hbm, wk_hbm, wv_hbm, rv_ref, logits_ref, x_ref, wq_ref, wk_ref, wv_ref, n_ref, q_ref, k_ref, sems
):
    @pl.when(lax.rem(lax.axis_index("aln"), 2) == 1)
    def _():
        pl.delay(STAGGER)

    copies = fetch(
        ((x_hbm, x_ref), (wq_hbm, wq_ref), (wk_hbm, wk_ref), (wv_hbm, wv_ref)), sems
    )
    tokens = x_ref.shape[0]
    positions = logits_ref.shape[1]
    sequences = tokens // positions
    first, count = lax.axis_index(SEQ) * sequences, tally[0]
    copies[0].wait()
    for s in range(sequences):
        part = slice(s * positions, (s + 1) * positions)
        n_ref[part, :] = standardize(x_ref[part, :].astype(F32)).astype(BF16)
    size = 2 * positions
    copies[1].wait()
    for start in range(0, tokens, size):
        part = slice(start, start + size)
        q = jnp.dot(n_ref[part, :], wq_ref[...], preferred_element_type=F32)
        for s in range(2):
            at = start + s * positions
            live = (first + at // positions < count).astype(F32)
            q_ref[at : at + positions, :] = (q[s * positions : (s + 1) * positions] * live).astype(BF16)
    copies[2].wait()
    for start in range(0, tokens, size):
        part = slice(start, start + size)
        k_ref[part, :] = jnp.dot(n_ref[part, :], wk_ref[...], preferred_element_type=F32).astype(BF16)
    copies[3].wait()
    for start in range(0, tokens, size):
        part = slice(start, start + size)
        rv_ref[part, :] = jnp.dot(n_ref[part, :], wv_ref[...], preferred_element_type=F32).astype(BF16)
    low, high = half_masks()
    for pair in range(H // 2):
        lanes = slice(pair * LANES, (pair + 1) * LANES)
        got = None
        for s in range(0, sequences, 2):
            rows = [slice((s + e) * positions, (s + e + 1) * positions) for e in range(2)]
            queries = jnp.concatenate([q_ref[r, lanes] for r in rows], axis=1)
            keys = [k_ref[r, lanes] for r in rows]
            even = jnp.concatenate([k * low for k in keys], axis=1)
            odd = jnp.concatenate([k * high for k in keys], axis=1)
            term = lax.dot_general(
                queries, jnp.concatenate([even, odd], axis=0), NT, preferred_element_type=F32
            )
            got = term if got is None else got + term
        at = 2 * pair * positions
        logits_ref[at : at + positions, :] = got[:, :positions].astype(BF16)
        logits_ref[at + positions : at + 2 * positions, :] = got[:, positions:].astype(BF16)


def weights_kernel(tally, parts_ref, out_ref):
    logits = parts_ref[0].astype(F32)
    for source in range(1, parts_ref.shape[0]):
        logits += parts_ref[source].astype(F32)
    count = jnp.full((1, 1), tally[0], jnp.int32).astype(F32)
    logits = logits / (jnp.sqrt(F32(DH)) * jnp.sqrt(count))
    top = jnp.max(logits, axis=-1, keepdims=True)
    powers = jnp.exp(logits - top)
    weights = (powers / jnp.sum(powers, axis=-1, keepdims=True)).astype(BF16)
    for target in range(out_ref.shape[0]):
        out_ref[target] = weights


def mix_kernel(tally, w_ref, rv_ref, x_ref, row_ref, send_ref, held):
    sequences, positions, width = held.shape
    first, count = lax.axis_index(SEQ) * sequences, tally[0]
    low, high = half_masks()
    for start in range(0, sequences, 2):
        mixed = [[], []]
        for pair in range(H // 2):
            at = 2 * pair * positions
            weights = jnp.concatenate(
                [w_ref[at : at + positions, :], w_ref[at + positions : at + 2 * positions, :]], axis=1
            )
            lanes = slice(pair * LANES, (pair + 1) * LANES)
            values = []
            for s in range(2):
                v = rv_ref[(start + s) * positions : (start + s + 1) * positions, lanes]
                values.append(jnp.concatenate([v * low, v * high], axis=0))
            got = jnp.dot(weights, jnp.concatenate(values, axis=1), preferred_element_type=F32)
            for s in range(2):
                mixed[s].append(lane_block(got, s))
        for s in range(2):
            live = (first + start + s < count).astype(F32)
            part = slice((start + s) * positions, (start + s + 1) * positions)
            out = (jnp.concatenate(mixed[s], axis=1) * live).astype(BF16)
            row_ref[part, :] = out
            held[start + s] = standardize(x_ref[part, :].astype(F32) + out.astype(F32))
    size = 16
    span = size * sequences
    for block in range(positions // size):
        turned = jnp.swapaxes(held[:, block * size : (block + 1) * size, :], 0, 1)
        send_ref[block * span : (block + 1) * span, :] = turned.reshape(span, width).astype(BF16)


def column_kernel(tally, n_ref, wq_ref, wk_ref, wv_ref, out_ref, q_ref, k_ref, v_ref):
    rows, width = n_ref.shape
    sets, columns, total, lanes = q_ref.shape
    factor = math.log2(math.e) / math.sqrt(DH)
    low, high = half_masks()
    lane = lax.broadcasted_iota(jnp.int32, (1, LANES), 1)
    is_low = lane < DH
    one_high = (lane == DH).astype(F32).astype(BF16)
    one_low = (lane == 0).astype(F32).astype(BF16)
    alive = lax.broadcasted_iota(jnp.int32, (total, 1), 0) < tally[0]
    bias = jnp.where(alive, 0.0, -1e30).astype(F32)
    bias_high = jnp.where(is_low, 0.0, bias).astype(BF16)
    bias_low = jnp.where(is_low, bias, 0.0).astype(BF16)
    live = alive.astype(F32)
    size = 256
    each = size // (8 * columns)

    def project(part, start, source, target, scale):
        got = jnp.dot(
            n_ref[start : start + size, :],
            source[:, part * lanes : (part + 1) * lanes],
            preferred_element_type=F32,
        )
        if scale is not None:
            got = got * scale
        got = got.reshape(each, columns, 8, lanes)
        at = start // columns
        for c in range(columns):
            target[part, c, at : at + each * 8, :] = got[:, c].reshape(each * 8, lanes).astype(BF16)

    def mix(q, k, v):
        scores = lax.dot_general(q, k, NT, preferred_element_type=F32)
        powers = jnp.exp2(scores - jnp.max(scores, axis=-1, keepdims=True)).astype(BF16)
        return jnp.dot(powers, v, preferred_element_type=F32)

    def attend(part, first, pair):
        outs = []
        span = slice(pair * LANES, (pair + 1) * LANES)
        for c in (first, first + 1):
            q, k, v = q_ref[part, c, :, span], k_ref[part, c, :, span], v_ref[part, c, :, span]
            even = mix(q * low + one_high, k * low + bias_high, v * low + high)
            odd = mix(q * high + one_low, k * high + bias_low, v * high + low)
            values = jnp.where(is_low, even, odd)
            sums = jnp.where(is_low, odd, even)
            outs.append((values * (live / pltpu.roll(sums, DH, 1))).reshape(total // 8, 8, LANES))
        at = part * lanes + pair * LANES
        both = jnp.stack(outs, axis=1).reshape(total // 8, 16, LANES)
        out_ref[:, first // 2, :, at : at + LANES] = both.astype(BF16)

    for part in range(sets):
        for start in range(0, rows, size):
            project(part, start, wq_ref, q_ref, factor)
            project(part, start, wk_ref, k_ref, None)
            project(part, start, wv_ref, v_ref, None)
        for first in range(0, columns, 2):
            for pair in range(lanes // LANES):
                attend(part, first, pair)


def call(kernel, tally, args, spaces, shapes, scratch, flops, name):
    specs = [pl.BlockSpec(memory_space=pltpu.SMEM)]
    return pl.pallas_call(
        kernel,
        in_specs=specs + [pl.BlockSpec(memory_space=s) for s in spaces],
        out_specs=[pl.BlockSpec(memory_space=pltpu.VMEM)] * len(shapes),
        out_shape=[jax.ShapeDtypeStruct(s, BF16) for s in shapes],
        scratch_shapes=scratch,
        cost_estimate=pl.CostEstimate(flops=flops, bytes_accessed=6 << 20, transcendentals=0),
        compiler_params=pltpu.CompilerParams(vmem_limit_bytes=24 << 20),
        name=name,
    )(tally, *args)


STAGGER = 20000


def exchange(value):
    return lax.all_to_all(value, SEQ, split_axis=0, concat_axis=0, tiled=True)


def local(x, tallies, hq, hk, hv, vq, vk, vv):
    sequences, positions, width = x.shape
    groups = lax.axis_size(SEQ)
    tokens = sequences * positions
    flat = x.reshape(tokens, width)
    share = H * positions // groups
    square = pltpu.VMEM((width, width), BF16)
    block = pltpu.VMEM((tokens, width), BF16)

    rv, logits = call(
        logits_kernel,
        tallies,
        tuple(pltpu.with_memory_space_constraint(a, pltpu.HBM) for a in (flat, hq, hk, hv)),
        [pltpu.HBM] * 4,
        [(tokens, width), (H * positions, positions)],
        [block, square, square, square, block, block, block, pltpu.SemaphoreType.DMA((4,))],
        6 * tokens * width * width,
        "row_logits",
    )
    parts = exchange(logits.reshape(groups, share, positions))
    (copies,) = call(
        weights_kernel,
        tallies,
        (parts,),
        [pltpu.VMEM],
        [(groups, share, positions)],
        [],
        1 << 20,
        "row_weights",
    )
    weights = exchange(copies).reshape(H * positions, positions)
    row_out, send = call(
        mix_kernel,
        tallies,
        (weights, rv, flat),
        [pltpu.VMEM] * 3,
        [(tokens, width)] * 2,
        [pltpu.VMEM((sequences, positions, width), F32)],
        4 * tokens * width * positions,
        "row_mix",
    )
    columns = positions // groups
    lanes = 2 * LANES
    got = exchange(send.reshape(groups, tokens // groups, width)).reshape(tokens, width)
    (out,) = call(
        column_kernel,
        tallies,
        (got, vq, vk, vv),
        [pltpu.VMEM] * 4,
        [(groups, columns // 2, 16, width)],
        [pltpu.VMEM((width // lanes, columns, tokens // columns, lanes), BF16)] * 3,
        6 * tokens * width * width,
        "columns",
    )
    back = exchange(out.reshape(groups, tokens // groups, width))
    result = jnp.swapaxes(back.reshape(positions, sequences, width), 0, 1)
    return row_out.reshape(sequences, positions, width), result


def solution(mesh):
    whole = P(("aln", "seq"), None, None)
    in_specs = (whole, P("aln"), P(), P(), P(), P(), P(), P())
    return jax.shard_map(
        local, mesh=mesh, in_specs=in_specs, out_specs=(whole, whole), check_vma=False
    )
```

time: 150 us -> 145 us (0.967)
  Pallas kernels: 50.5 us -> 39.2 us
  blocking collectives: 96.4 us -> 103 us
    pallas_call x4, Pallas kernels: 50.5 us -> 39.2 us  [call(): pl.pallas_call(kernel, in_specs=specs + [pl.BlockSpec(memory_space=s) for...]
    all_to_all x4, blocking collectives: 96.4 us -> 103 us  [exchange(): return lax.all_to_all(value, SEQ, split_axis=0, concat_axis=0, tiled=True)]
where the time goes in v3:
time: 145 us
  blocking collectives  103 us (71%)
  Pallas kernels  39.2 us (27%)
  local copies, waits for them, and re-layouts  1.45 us (1%)
    all_to_all x4, blocking collectives, exchange(): return lax.all_to_all(value, SEQ, split_axis=0, concat_axis=0, tiled=True)  103 us
    pallas_call x4, Pallas kernels, call(): pl.pallas_call(kernel, in_specs=specs + [pl.BlockSpec(memory_space=s) for...  39.2 us

profile of v3, /device:TPU:1, one launch (start us, length us, event | category | flops | bytes accessed | tf_op | source)
XLA Modules:
  0.0 144.7 jit_solution(17762740517068619014)
XLA Ops:
  1.3 27.5 %row_logits.1 = (bf16[1024,768]{1,0:T(8,128)(2,1)S(1)}, bf16[1536,128]{1,0:T(8,128)(2,1)S(1)}) custom-call(s32[1]{0:T(128)S(6)} %copy.11.tally, bf16[1024,768]{1,0:T(8,128)(2,1)} %bitcast.13, bf16[768,768]{1,0:T(8,128)(2,1)} %wq_hbm.1, bf16[768,768]{1,0:T(8,128)(2,1)} %wk_hbm.1, bf16[768,768]{1,0:T(8,128)(2,1)} %wv_hbm.1), custom_call_target="tpu_custom_call" | custom-call | flops 3623878656 | bytes 6291456 | tf_op jit(solution)/shard_map/row_logits/pallas_call | solution.py:204
  28.7 0.0 copy-start
  28.8 25.9 %all_to_all.20.parts_ref = bf16[32,48,128]{2,1,0:T(8,128)(2,1)S(1)} all-to-all(bf16[32,48,128]{2,1,0:T(8,128)(2,1)S(1)} %bitcast.16), channel_id=1, replica_groups=mesh['aln'=8,'seq'=32] {'seq'}, dimensions={0} | all-to-all | bytes 786432 | tf_op jit(solution)/shard_map/all_to_all | solution.py:220
  54.6 0.2 row_weights.1
  54.9 15.8 %all_to_all.21 = bf16[32,48,128]{2,1,0:T(8,128)(2,1)S(1)} all-to-all(bf16[32,48,128]{2,1,0:T(8,128)(2,1)S(1)} %row_weights.1), channel_id=1, replica_groups=mesh['aln'=8,'seq'=32] {'seq'}, dimensions={0} | all-to-all | bytes 786432 | tf_op jit(solution)/shard_map/all_to_all | solution.py:220
  70.7 0.0 copy-done
  70.7 0.0 copy-start.3
  70.7 2.8 %row_mix.1 = (bf16[1024,768]{1,0:T(8,128)(2,1)}, bf16[1024,768]{1,0:T(8,128)(2,1)S(1)}) custom-call(s32[1]{0:T(128)S(6)} %copy.11.tally, bf16[1536,128]{1,0:T(8,128)(2,1)S(1)} %bitcast.15, bf16[1024,768]{1,0:T(8,128)(2,1)S(1)} %get-tuple-element.7.rv_ref, bf16[1024,768]{1,0:T(8,128)(2,1)S(1)} %bitcast.14), custom_call_target="tpu_custom_call" | custom-call | flops 402653184 | bytes 6291456 | tf_op jit(solution)/shard_map/row_mix/pallas_call | solution.py:204
  73.4 0.0 copy-start.1
  73.4 0.0 copy-start.2
  73.5 30.3 %all_to_all.22 = bf16[32,32,768]{2,1,0:T(8,128)(2,1)S(1)} all-to-all(bf16[32,32,768]{2,1,0:T(8,128)(2,1)S(1)} %bitcast.10), channel_id=1, replica_groups=mesh['aln'=8,'seq'=32] {'seq'}, dimensions={0} | all-to-all | bytes 3145728 | tf_op jit(solution)/shard_map/all_to_all | solution.py:220
  103.7 0.0 copy-done.3
  103.7 0.0 copy-done.1
  103.7 0.0 copy-done.2
  103.7 8.7 %columns.1 = bf16[32,2,16,768]{3,2,1,0:T(8,128)(2,1)S(1)} custom-call(s32[1]{0:T(128)S(6)} %copy.11.tally, bf16[1024,768]{1,0:T(8,128)(2,1)S(1)} %bitcast.11, bf16[768,768]{1,0:T(8,128)(2,1)S(1)} %copy-done.1, bf16[768,768]{1,0:T(8,128)(2,1)S(1)} %copy-done.2, bf16[768,768]{1,0:T(8,128)(2,1)S(1)} %copy-done.3), custom_call_target="tpu_custom_call" | custom-call | flops 3623878656 | bytes 6291456 | tf_op jit(solution)/shard_map/columns/pallas_call | solution.py:204
  112.5 30.8 %all_to_all.23 = bf16[32,32,768]{2,1,0:T(8,128)(2,1)S(1)} all-to-all(bf16[32,32,768]{2,1,0:T(8,128)(2,1)S(1)} %bitcast.12), channel_id=1, replica_groups=mesh['aln'=8,'seq'=32] {'seq'}, dimensions={0} | all-to-all | bytes 3145728 | tf_op jit(solution)/shard_map/all_to_all | solution.py:220
  143.3 1.4 copy.10
Async XLA Ops:
  28.7 41.9 %copy-start = (bf16[8,128,768]{2,1,0:T(8,128)(2,1)S(1)}, bf16[8,128,768]{2,1,0:T(8,128)(2,1)}, u32[]{:S(2)}) copy-start(bf16[8,128,768]{2,1,0:T(8,128)(2,1)} %param.8) | copy-start | bytes 4718596
  70.7 33.0 %copy-start.3 = (bf16[768,768]{1,0:T(8,128)(2,1)S(1)}, bf16[768,768]{1,0:T(8,128)(2,1)}, u32[]{:S(2)}) copy-start(bf16[768,768]{1,0:T(8,128)(2,1)} %wv_ref.1) | copy-start | bytes 3538948
  73.4 30.3 %copy-start.1 = (bf16[768,768]{1,0:T(8,128)(2,1)S(1)}, bf16[768,768]{1,0:T(8,128)(2,1)}, u32[]{:S(2)}) copy-start(bf16[768,768]{1,0:T(8,128)(2,1)} %wq_ref.1) | copy-start | bytes 3538948
  73.4 30.3 %copy-start.2 = (bf16[768,768]{1,0:T(8,128)(2,1)S(1)}, bf16[768,768]{1,0:T(8,128)(2,1)}, u32[]{:S(2)}) copy-start(bf16[768,768]{1,0:T(8,128)(2,1)} %wk_ref.1) | copy-start | bytes 3538948

commit v4 on v3

--- a/solution.py
+++ b/solution.py
@@ -34,6 +34,12 @@
     return value[:, index * LANES : (index + 1) * LANES]
 
 
+def hold_second_core(duration):
+    @pl.when(lax.rem(lax.axis_index("aln"), 2) == 1)
+    def _():
+        pl.delay(duration)
+
+
 def fetch(refs, sems):
     copies = [pltpu.make_async_copy(src, dst, sems.at[i]) for i, (src, dst) in enumerate(refs)]
     for copy in copies:
@@ -44,10 +50,7 @@
 def logits_kernel(
     tally, x_hbm, wq_hbm, wk_hbm, wv_hbm, rv_ref, logits_ref, x_ref, wq_ref, wk_ref, wv_ref, n_ref, q_ref, k_ref, sems
 ):
-    @pl.when(lax.rem(lax.axis_index("aln"), 2) == 1)
-    def _():
-        pl.delay(STAGGER)
-
+    hold_second_core(FIRST_STAGGER)
     copies = fetch(
         ((x_hbm, x_ref), (wq_hbm, wq_ref), (wk_hbm, wk_ref), (wv_hbm, wv_ref)), sems
     )
@@ -109,6 +112,7 @@
 
 
 def mix_kernel(tally, w_ref, rv_ref, x_ref, row_ref, send_ref, held):
+    hold_second_core(SECOND_STAGGER)
     sequences, positions, width = held.shape
     first, count = lax.axis_index(SEQ) * sequences, tally[0]
     low, high = half_masks()
@@ -213,7 +217,8 @@
     )(tally, *args)
 
 
-STAGGER = 20000
+FIRST_STAGGER = 10500
+SECOND_STAGGER = 11500
 
 
 def exchange(value):

time: 145 us -> 139 us (0.959)
  blocking collectives: 103 us -> 95 us
  Pallas kernels: 39.2 us -> 41.2 us
    all_to_all x4, blocking collectives: 103 us -> 95 us  [exchange(): return lax.all_to_all(value, SEQ, split_axis=0, concat_axis=0, tiled=True)]
    pallas_call x4, Pallas kernels: 39.2 us -> 41.2 us  [call(): pl.pallas_call(kernel, in_specs=specs + [pl.BlockSpec(memory_space=s) for...]
where the time goes in v4:
time: 139 us
  blocking collectives  95 us (68%)
  Pallas kernels  41.2 us (30%)
  local copies, waits for them, and re-layouts  1.45 us (1%)
    all_to_all x4, blocking collectives, exchange(): return lax.all_to_all(value, SEQ, split_axis=0, concat_axis=0, tiled=True)  95 us
    pallas_call x4, Pallas kernels, call(): pl.pallas_call(kernel, in_specs=specs + [pl.BlockSpec(memory_space=s) for...  41.2 us

profile of v4, /device:TPU:1, one launch (start us, length us, event | category | flops | bytes accessed | tf_op | source)
XLA Modules:
  0.0 139.0 jit_solution(1583347587747724858)
XLA Ops:
  1.3 18.0 %row_logits.1 = (bf16[1024,768]{1,0:T(8,128)(2,1)S(1)}, bf16[1536,128]{1,0:T(8,128)(2,1)S(1)}) custom-call(s32[1]{0:T(128)S(6)} %copy.11.tally, bf16[1024,768]{1,0:T(8,128)(2,1)} %bitcast.13, bf16[768,768]{1,0:T(8,128)(2,1)} %wq_hbm.1, bf16[768,768]{1,0:T(8,128)(2,1)} %wk_hbm.1, bf16[768,768]{1,0:T(8,128)(2,1)} %wv_hbm.1), custom_call_target="tpu_custom_call" | custom-call | flops 3623878656 | bytes 6291456 | tf_op jit(solution)/shard_map/row_logits/pallas_call | solution.py:208
  19.2 0.0 copy-start
  19.3 23.5 %all_to_all.20.parts_ref = bf16[32,48,128]{2,1,0:T(8,128)(2,1)S(1)} all-to-all(bf16[32,48,128]{2,1,0:T(8,128)(2,1)S(1)} %bitcast.16), channel_id=1, replica_groups=mesh['aln'=8,'seq'=32] {'seq'}, dimensions={0} | all-to-all | bytes 786432 | tf_op jit(solution)/shard_map/all_to_all | solution.py:225
  42.7 0.2 row_weights.1
  43.0 15.1 %all_to_all.21 = bf16[32,48,128]{2,1,0:T(8,128)(2,1)S(1)} all-to-all(bf16[32,48,128]{2,1,0:T(8,128)(2,1)S(1)} %row_weights.1), channel_id=1, replica_groups=mesh['aln'=8,'seq'=32] {'seq'}, dimensions={0} | all-to-all | bytes 786432 | tf_op jit(solution)/shard_map/all_to_all | solution.py:225
  58.1 0.0 copy-done
  58.1 0.0 copy-start.3
  58.1 14.3 %row_mix.1 = (bf16[1024,768]{1,0:T(8,128)(2,1)}, bf16[1024,768]{1,0:T(8,128)(2,1)S(1)}) custom-call(s32[1]{0:T(128)S(6)} %copy.11.tally, bf16[1536,128]{1,0:T(8,128)(2,1)S(1)} %bitcast.15, bf16[1024,768]{1,0:T(8,128)(2,1)S(1)} %get-tuple-element.7.rv_ref, bf16[1024,768]{1,0:T(8,128)(2,1)S(1)} %bitcast.14), custom_call_target="tpu_custom_call" | custom-call | flops 402653184 | bytes 6291456 | tf_op jit(solution)/shard_map/row_mix/pallas_call | solution.py:208
  72.3 0.0 copy-start.1
  72.3 0.0 copy-start.2
  72.3 27.7 %all_to_all.22 = bf16[32,32,768]{2,1,0:T(8,128)(2,1)S(1)} all-to-all(bf16[32,32,768]{2,1,0:T(8,128)(2,1)S(1)} %bitcast.10), channel_id=1, replica_groups=mesh['aln'=8,'seq'=32] {'seq'}, dimensions={0} | all-to-all | bytes 3145728 | tf_op jit(solution)/shard_map/all_to_all | solution.py:225
  100.1 0.0 copy-done.3
  100.1 0.0 copy-done.1
  100.1 0.0 copy-done.2
  100.1 8.7 %columns.1 = bf16[32,2,16,768]{3,2,1,0:T(8,128)(2,1)S(1)} custom-call(s32[1]{0:T(128)S(6)} %copy.11.tally, bf16[1024,768]{1,0:T(8,128)(2,1)S(1)} %bitcast.11, bf16[768,768]{1,0:T(8,128)(2,1)S(1)} %copy-done.1, bf16[768,768]{1,0:T(8,128)(2,1)S(1)} %copy-done.2, bf16[768,768]{1,0:T(8,128)(2,1)S(1)} %copy-done.3), custom_call_target="tpu_custom_call" | custom-call | flops 3623878656 | bytes 6291456 | tf_op jit(solution)/shard_map/columns/pallas_call | solution.py:208
  108.8 28.7 %all_to_all.23 = bf16[32,32,768]{2,1,0:T(8,128)(2,1)S(1)} all-to-all(bf16[32,32,768]{2,1,0:T(8,128)(2,1)S(1)} %bitcast.12), channel_id=1, replica_groups=mesh['aln'=8,'seq'=32] {'seq'}, dimensions={0} | all-to-all | bytes 3145728 | tf_op jit(solution)/shard_map/all_to_all | solution.py:225
  137.5 1.4 %copy.10 = bf16[8,128,768]{2,1,0:T(8,128)(2,1)} copy(bf16[8,128,768]{2,0,1:T(8,128)(2,1)S(1)} %bitcast.17) | data formatting | bytes 3145728
Async XLA Ops:
  19.2 38.8 %copy-start = (bf16[8,128,768]{2,1,0:T(8,128)(2,1)S(1)}, bf16[8,128,768]{2,1,0:T(8,128)(2,1)}, u32[]{:S(2)}) copy-start(bf16[8,128,768]{2,1,0:T(8,128)(2,1)} %param.8) | copy-start | bytes 4718596
  58.1 42.0 %copy-start.3 = (bf16[768,768]{1,0:T(8,128)(2,1)S(1)}, bf16[768,768]{1,0:T(8,128)(2,1)}, u32[]{:S(2)}) copy-start(bf16[768,768]{1,0:T(8,128)(2,1)} %wv_ref.1) | copy-start | bytes 3538948
  72.3 27.7 %copy-start.1 = (bf16[768,768]{1,0:T(8,128)(2,1)S(1)}, bf16[768,768]{1,0:T(8,128)(2,1)}, u32[]{:S(2)}) copy-start(bf16[768,768]{1,0:T(8,128)(2,1)} %wq_ref.1) | copy-start | bytes 3538948
  72.3 27.8 %copy-start.2 = (bf16[768,768]{1,0:T(8,128)(2,1)S(1)}, bf16[768,768]{1,0:T(8,128)(2,1)}, u32[]{:S(2)}) copy-start(bf16[768,768]{1,0:T(8,128)(2,1)} %wk_ref.1) | copy-start | bytes 3538948

commit v5 on v4

--- a/solution.py
+++ b/solution.py
@@ -51,51 +51,69 @@
     tally, x_hbm, wq_hbm, wk_hbm, wv_hbm, rv_ref, logits_ref, x_ref, wq_ref, wk_ref, wv_ref, n_ref, q_ref, k_ref, sems
 ):
     hold_second_core(FIRST_STAGGER)
-    copies = fetch(
-        ((x_hbm, x_ref), (wq_hbm, wq_ref), (wk_hbm, wk_ref), (wv_hbm, wv_ref)), sems
-    )
     tokens = x_ref.shape[0]
     positions = logits_ref.shape[1]
     sequences = tokens // positions
     first, count = lax.axis_index(SEQ) * sequences, tally[0]
-    copies[0].wait()
-    for s in range(sequences):
-        part = slice(s * positions, (s + 1) * positions)
+    early, late = pl.ds(0, tokens // 2), pl.ds(tokens // 2, tokens // 2)
+    copies = fetch(
+        (
+            (x_hbm.at[early], x_ref.at[early]),
+            (wq_hbm, wq_ref),
+            (x_hbm.at[late], x_ref.at[late]),
+            (wk_hbm, wk_ref),
+            (wv_hbm, wv_ref),
+        ),
+        sems,
+    )
+    size = 2 * positions
+    blocks = [slice(start, start + size) for start in range(0, tokens, size)]
+
+    def norm(part):
         n_ref[part, :] = standardize(x_ref[part, :].astype(F32)).astype(BF16)
-    size = 2 * positions
-    copies[1].wait()
-    for start in range(0, tokens, size):
-        part = slice(start, start + size)
+
+    def query(part):
         q = jnp.dot(n_ref[part, :], wq_ref[...], preferred_element_type=F32)
         for s in range(2):
-            at = start + s * positions
+            at = part.start + s * positions
             live = (first + at // positions < count).astype(F32)
             q_ref[at : at + positions, :] = (q[s * positions : (s + 1) * positions] * live).astype(BF16)
+
+    def plain(part, source, target):
+        target[part, :] = jnp.dot(n_ref[part, :], source[...], preferred_element_type=F32).astype(BF16)
+
+    half = len(blocks) // 2
+    copies[0].wait()
+    for part in blocks[:half]:
+        norm(part)
+    copies[1].wait()
     copies[2].wait()
-    for start in range(0, tokens, size):
-        part = slice(start, start + size)
-        k_ref[part, :] = jnp.dot(n_ref[part, :], wk_ref[...], preferred_element_type=F32).astype(BF16)
+    for at, part in enumerate(blocks):
+        query(part)
+        if at < half:
+            norm(blocks[half + at])
     copies[3].wait()
-    for start in range(0, tokens, size):
-        part = slice(start, start + size)
-        rv_ref[part, :] = jnp.dot(n_ref[part, :], wv_ref[...], preferred_element_type=F32).astype(BF16)
+    copies[4].wait()
+    for part in blocks:
+        plain(part, wk_ref, k_ref)
+    for part in blocks:
+        plain(part, wv_ref, rv_ref)
     low, high = half_masks()
     for pair in range(H // 2):
         lanes = slice(pair * LANES, (pair + 1) * LANES)
         got = None
         for s in range(0, sequences, 2):
             rows = [slice((s + e) * positions, (s + e + 1) * positions) for e in range(2)]
-            queries = jnp.concatenate([q_ref[r, lanes] for r in rows], axis=1)
-            keys = [k_ref[r, lanes] for r in rows]
-            even = jnp.concatenate([k * low for k in keys], axis=1)
-            odd = jnp.concatenate([k * high for k in keys], axis=1)
+            queries = [q_ref[r, lanes] for r in rows]
+            even = jnp.concatenate([q * low for q in queries], axis=1)
+            odd = jnp.concatenate([q * high for q in queries], axis=1)
+            keys = jnp.concatenate([k_ref[r, lanes] for r in rows], axis=1)
             term = lax.dot_general(
-                queries, jnp.concatenate([even, odd], axis=0), NT, preferred_element_type=F32
+                jnp.concatenate([even, odd], axis=0), keys, NT, preferred_element_type=F32
             )
             got = term if got is None else got + term
         at = 2 * pair * positions
-        logits_ref[at : at + positions, :] = got[:, :positions].astype(BF16)
-        logits_ref[at + positions : at + 2 * positions, :] = got[:, positions:].astype(BF16)
+        logits_ref[at : at + 2 * positions, :] = got.astype(BF16)
 
 
 def weights_kernel(tally, parts_ref, out_ref):
@@ -240,7 +258,7 @@
         tuple(pltpu.with_memory_space_constraint(a, pltpu.HBM) for a in (flat, hq, hk, hv)),
         [pltpu.HBM] * 4,
         [(tokens, width), (H * positions, positions)],
-        [block, square, square, square, block, block, block, pltpu.SemaphoreType.DMA((4,))],
+        [block, square, square, square, block, block, block, pltpu.SemaphoreType.DMA((5,))],
         6 * tokens * width * width,
         "row_logits",
     )

time: 139 us -> 138 us (level)
  no operation moved by 1% of the time
where the time goes in v5:
time: 138 us
  blocking collectives  95 us (69%)
  Pallas kernels  40.3 us (29%)
  local copies, waits for them, and re-layouts  1.45 us (1%)
    all_to_all x4, blocking collectives, exchange(): return lax.all_to_all(value, SEQ, split_axis=0, concat_axis=0, tiled=True)  95 us
    pallas_call x4, Pallas kernels, call(): pl.pallas_call(kernel, in_specs=specs + [pl.BlockSpec(memory_space=s) for...  40.3 us

profile of v5, /device:TPU:1, one launch (start us, length us, event | category | flops | bytes accessed | tf_op | source)
XLA Modules:
  0.0 138.1 jit_solution(15804100684650008761)
XLA Ops:
  1.3 17.1 %row_logits.1 = (bf16[1024,768]{1,0:T(8,128)(2,1)S(1)}, bf16[1536,128]{1,0:T(8,128)(2,1)S(1)}) custom-call(s32[1]{0:T(128)S(6)} %copy.11.tally, bf16[1024,768]{1,0:T(8,128)(2,1)} %bitcast.13, bf16[768,768]{1,0:T(8,128)(2,1)} %wq_hbm.1, bf16[768,768]{1,0:T(8,128)(2,1)} %wk_hbm.1, bf16[768,768]{1,0:T(8,128)(2,1)} %wv_hbm.1), custom_call_target="tpu_custom_call" | custom-call | flops 3623878656 | bytes 6291456 | tf_op jit(solution)/shard_map/row_logits/pallas_call | solution.py:226
  18.4 0.0 copy-start
  18.4 23.5 %all_to_all.20.parts_ref = bf16[32,48,128]{2,1,0:T(8,128)(2,1)S(1)} all-to-all(bf16[32,48,128]{2,1,0:T(8,128)(2,1)S(1)} %bitcast.16), channel_id=1, replica_groups=mesh['aln'=8,'seq'=32] {'seq'}, dimensions={0} | all-to-all | bytes 786432 | tf_op jit(solution)/shard_map/all_to_all | solution.py:243
  41.9 0.2 row_weights.1
  42.1 15.1 %all_to_all.21 = bf16[32,48,128]{2,1,0:T(8,128)(2,1)S(1)} all-to-all(bf16[32,48,128]{2,1,0:T(8,128)(2,1)S(1)} %row_weights.1), channel_id=1, replica_groups=mesh['aln'=8,'seq'=32] {'seq'}, dimensions={0} | all-to-all | bytes 786432 | tf_op jit(solution)/shard_map/all_to_all | solution.py:243
  57.2 0.0 copy-done
  57.2 0.0 copy-start.3
  57.2 14.3 %row_mix.1 = (bf16[1024,768]{1,0:T(8,128)(2,1)}, bf16[1024,768]{1,0:T(8,128)(2,1)S(1)}) custom-call(s32[1]{0:T(128)S(6)} %copy.11.tally, bf16[1536,128]{1,0:T(8,128)(2,1)S(1)} %bitcast.15, bf16[1024,768]{1,0:T(8,128)(2,1)S(1)} %get-tuple-element.7.rv_ref, bf16[1024,768]{1,0:T(8,128)(2,1)S(1)} %bitcast.14), custom_call_target="tpu_custom_call" | custom-call | flops 402653184 | bytes 6291456 | tf_op jit(solution)/shard_map/row_mix/pallas_call | solution.py:226
  71.5 0.0 copy-start.1
  71.5 0.0 copy-start.2
  71.5 27.7 %all_to_all.22 = bf16[32,32,768]{2,1,0:T(8,128)(2,1)S(1)} all-to-all(bf16[32,32,768]{2,1,0:T(8,128)(2,1)S(1)} %bitcast.10), channel_id=1, replica_groups=mesh['aln'=8,'seq'=32] {'seq'}, dimensions={0} | all-to-all | bytes 3145728 | tf_op jit(solution)/shard_map/all_to_all | solution.py:243
  99.2 0.0 copy-done.3
  99.2 0.0 copy-done.1
  99.3 0.0 copy-done.2
  99.3 8.7 %columns.1 = bf16[32,2,16,768]{3,2,1,0:T(8,128)(2,1)S(1)} custom-call(s32[1]{0:T(128)S(6)} %copy.11.tally, bf16[1024,768]{1,0:T(8,128)(2,1)S(1)} %bitcast.11, bf16[768,768]{1,0:T(8,128)(2,1)S(1)} %copy-done.1, bf16[768,768]{1,0:T(8,128)(2,1)S(1)} %copy-done.2, bf16[768,768]{1,0:T(8,128)(2,1)S(1)} %copy-done.3), custom_call_target="tpu_custom_call" | custom-call | flops 3623878656 | bytes 6291456 | tf_op jit(solution)/shard_map/columns/pallas_call | solution.py:226
  108.0 28.7 %all_to_all.23 = bf16[32,32,768]{2,1,0:T(8,128)(2,1)S(1)} all-to-all(bf16[32,32,768]{2,1,0:T(8,128)(2,1)S(1)} %bitcast.12), channel_id=1, replica_groups=mesh['aln'=8,'seq'=32] {'seq'}, dimensions={0} | all-to-all | bytes 3145728 | tf_op jit(solution)/shard_map/all_to_all | solution.py:243
  136.7 1.4 %copy.10 = bf16[8,128,768]{2,1,0:T(8,128)(2,1)} copy(bf16[8,128,768]{2,0,1:T(8,128)(2,1)S(1)} %bitcast.17) | data formatting | bytes 3145728
Async XLA Ops:
  18.4 38.8 %copy-start = (bf16[8,128,768]{2,1,0:T(8,128)(2,1)S(1)}, bf16[8,128,768]{2,1,0:T(8,128)(2,1)}, u32[]{:S(2)}) copy-start(bf16[8,128,768]{2,1,0:T(8,128)(2,1)} %param.8) | copy-start | bytes 4718596
  57.2 42.0 %copy-start.3 = (bf16[768,768]{1,0:T(8,128)(2,1)S(1)}, bf16[768,768]{1,0:T(8,128)(2,1)}, u32[]{:S(2)}) copy-start(bf16[768,768]{1,0:T(8,128)(2,1)} %wv_ref.1) | copy-start | bytes 3538948
  71.5 27.7 %copy-start.1 = (bf16[768,768]{1,0:T(8,128)(2,1)S(1)}, bf16[768,768]{1,0:T(8,128)(2,1)}, u32[]{:S(2)}) copy-start(bf16[768,768]{1,0:T(8,128)(2,1)} %wq_ref.1) | copy-start | bytes 3538948
  71.5 27.8 %copy-start.2 = (bf16[768,768]{1,0:T(8,128)(2,1)S(1)}, bf16[768,768]{1,0:T(8,128)(2,1)}, u32[]{:S(2)}) copy-start(bf16[768,768]{1,0:T(8,128)(2,1)} %wk_ref.1) | copy-start | bytes 3538948

commit v6 on v5

--- a/solution.py
+++ b/solution.py
@@ -221,6 +221,22 @@
                 attend(part, first, pair)
 
 
+def turn_kernel(recv_ref, out_hbm, held, sems):
+    sequences, positions, width = held.shape
+    size = 16
+    copies = []
+    for block in range(positions // size):
+        part = pl.ds(block * size, size)
+        got = recv_ref[block * size * sequences : (block + 1) * size * sequences, :].astype(F32)
+        turned = jnp.swapaxes(got.reshape(size, sequences, width), 0, 1)
+        held[:, block * size : (block + 1) * size, :] = turned.astype(BF16)
+        copy = pltpu.make_async_copy(held.at[:, part, :], out_hbm.at[:, part, :], sems.at[block])
+        copy.start()
+        copies.append(copy)
+    for copy in copies:
+        copy.wait()
+
+
 def call(kernel, tally, args, spaces, shapes, scratch, flops, name):
     specs = [pl.BlockSpec(memory_space=pltpu.SMEM)]
     return pl.pallas_call(
@@ -298,7 +314,19 @@
         "columns",
     )
     back = exchange(out.reshape(groups, tokens // groups, width))
-    result = jnp.swapaxes(back.reshape(positions, sequences, width), 0, 1)
+    result = pl.pallas_call(
+        turn_kernel,
+        in_specs=[pl.BlockSpec(memory_space=pltpu.VMEM)],
+        out_specs=pl.BlockSpec(memory_space=pltpu.HBM),
+        out_shape=jax.ShapeDtypeStruct((sequences, positions, width), BF16),
+        scratch_shapes=[
+            pltpu.VMEM((sequences, positions, width), BF16),
+            pltpu.SemaphoreType.DMA((positions // 16,)),
+        ],
+        cost_estimate=pl.CostEstimate(flops=0, bytes_accessed=3 << 20, transcendentals=0),
+        compiler_params=pltpu.CompilerParams(vmem_limit_bytes=24 << 20),
+        name="turn_back",
+    )(back.reshape(tokens, width))
     return row_out.reshape(sequences, positions, width), result
 
 

time: 138 us -> 139 us (level)
  Pallas kernels: 40.3 us -> 41.9 us
  local copies, waits for them, and re-layouts: 1.45 us -> 0.02 us
    pallas_call x0 -> x1, Pallas kernels: none -> 1.53 us  [local(): pl.pallas_call(turn_kernel, in_specs=[pl.BlockSpec(memory_space=pltpu.VME...]
    unnamed x9 -> x8, local copies, waits for them, and re-layouts: 1.45 us -> 0.02 us
where the time goes in v6:
time: 139 us; the launch traced here: 138 us
  blocking collectives  95 us (68%)
  Pallas kernels  41.9 us (30%)
  between operations  1.47 us (1%)
    all_to_all x4, blocking collectives, exchange(): return lax.all_to_all(value, SEQ, split_axis=0, concat_axis=0, tiled=True)  95 us
    pallas_call x4, Pallas kernels, call(): pl.pallas_call(kernel, in_specs=specs + [pl.BlockSpec(memory_space=s) for...  40.3 us

profile of v6, /device:TPU:1, one launch (start us, length us, event | category | flops | bytes accessed | tf_op | source)
XLA Modules:
  0.0 138.4 jit_solution(13764340273776287254)
XLA Ops:
  1.3 17.1 %row_logits.1 = (bf16[1024,768]{1,0:T(8,128)(2,1)S(1)}, bf16[1536,128]{1,0:T(8,128)(2,1)S(1)}) custom-call(s32[1]{0:T(128)S(6)} %copy.10.tally, bf16[1024,768]{1,0:T(8,128)(2,1)} %bitcast.12, bf16[768,768]{1,0:T(8,128)(2,1)} %wq_hbm.1, bf16[768,768]{1,0:T(8,128)(2,1)} %wk_hbm.1, bf16[768,768]{1,0:T(8,128)(2,1)} %wv_hbm.1), custom_call_target="tpu_custom_call" | custom-call | flops 3623878656 | bytes 6291456 | tf_op jit(solution)/shard_map/row_logits/pallas_call | solution.py:242
  18.4 0.0 copy-start
  18.4 23.5 %all_to_all.20.parts_ref = bf16[32,48,128]{2,1,0:T(8,128)(2,1)S(1)} all-to-all(bf16[32,48,128]{2,1,0:T(8,128)(2,1)S(1)} %bitcast.15), channel_id=1, replica_groups=mesh['aln'=8,'seq'=32] {'seq'}, dimensions={0} | all-to-all | bytes 786432 | tf_op jit(solution)/shard_map/all_to_all | solution.py:259
  41.9 0.2 row_weights.1
  42.1 15.1 %all_to_all.21 = bf16[32,48,128]{2,1,0:T(8,128)(2,1)S(1)} all-to-all(bf16[32,48,128]{2,1,0:T(8,128)(2,1)S(1)} %row_weights.1), channel_id=1, replica_groups=mesh['aln'=8,'seq'=32] {'seq'}, dimensions={0} | all-to-all | bytes 786432 | tf_op jit(solution)/shard_map/all_to_all | solution.py:259
  57.2 0.0 copy-done
  57.2 0.0 copy-start.3
  57.2 14.3 %row_mix.1 = (bf16[1024,768]{1,0:T(8,128)(2,1)}, bf16[1024,768]{1,0:T(8,128)(2,1)S(1)}) custom-call(s32[1]{0:T(128)S(6)} %copy.10.tally, bf16[1536,128]{1,0:T(8,128)(2,1)S(1)} %bitcast.14, bf16[1024,768]{1,0:T(8,128)(2,1)S(1)} %get-tuple-element.7.rv_ref, bf16[1024,768]{1,0:T(8,128)(2,1)S(1)} %bitcast.13), custom_call_target="tpu_custom_call" | custom-call | flops 402653184 | bytes 6291456 | tf_op jit(solution)/shard_map/row_mix/pallas_call | solution.py:242
  71.5 0.0 copy-start.1
  71.5 0.0 copy-start.2
  71.5 27.7 %all_to_all.22 = bf16[32,32,768]{2,1,0:T(8,128)(2,1)S(1)} all-to-all(bf16[32,32,768]{2,1,0:T(8,128)(2,1)S(1)} %bitcast.9), channel_id=1, replica_groups=mesh['aln'=8,'seq'=32] {'seq'}, dimensions={0} | all-to-all | bytes 3145728 | tf_op jit(solution)/shard_map/all_to_all | solution.py:259
  99.2 0.0 copy-done.3
  99.2 0.0 copy-done.1
  99.3 0.0 copy-done.2
  99.3 8.7 %columns.1 = bf16[32,2,16,768]{3,2,1,0:T(8,128)(2,1)S(1)} custom-call(s32[1]{0:T(128)S(6)} %copy.10.tally, bf16[1024,768]{1,0:T(8,128)(2,1)S(1)} %bitcast.10, bf16[768,768]{1,0:T(8,128)(2,1)S(1)} %copy-done.1, bf16[768,768]{1,0:T(8,128)(2,1)S(1)} %copy-done.2, bf16[768,768]{1,0:T(8,128)(2,1)S(1)} %copy-done.3), custom_call_target="tpu_custom_call" | custom-call | flops 3623878656 | bytes 6291456 | tf_op jit(solution)/shard_map/columns/pallas_call | solution.py:242
  108.0 28.7 %all_to_all.23 = bf16[32,32,768]{2,1,0:T(8,128)(2,1)S(1)} all-to-all(bf16[32,32,768]{2,1,0:T(8,128)(2,1)S(1)} %bitcast.11), channel_id=1, replica_groups=mesh['aln'=8,'seq'=32] {'seq'}, dimensions={0} | all-to-all | bytes 3145728 | tf_op jit(solution)/shard_map/all_to_all | solution.py:259
  136.7 1.5 %turn_back.1 = bf16[8,128,768]{2,1,0:T(8,128)(2,1)} custom-call(bf16[1024,768]{1,0:T(8,128)(2,1)S(1)} %bitcast.8), custom_call_target="tpu_custom_call" | custom-call | bytes 3145728 | tf_op jit(solution)/shard_map/turn_back/pallas_call | solution.py:317
Async XLA Ops:
  18.4 38.8 %copy-start = (bf16[8,128,768]{2,1,0:T(8,128)(2,1)S(1)}, bf16[8,128,768]{2,1,0:T(8,128)(2,1)}, u32[]{:S(2)}) copy-start(bf16[8,128,768]{2,1,0:T(8,128)(2,1)} %param.8) | copy-start | bytes 4718596
  57.2 42.0 %copy-start.3 = (bf16[768,768]{1,0:T(8,128)(2,1)S(1)}, bf16[768,768]{1,0:T(8,128)(2,1)}, u32[]{:S(2)}) copy-start(bf16[768,768]{1,0:T(8,128)(2,1)} %wv_ref.1) | copy-start | bytes 3538948
  71.5 27.7 %copy-start.1 = (bf16[768,768]{1,0:T(8,128)(2,1)S(1)}, bf16[768,768]{1,0:T(8,128)(2,1)}, u32[]{:S(2)}) copy-start(bf16[768,768]{1,0:T(8,128)(2,1)} %wq_ref.1) | copy-start | bytes 3538948
  71.5 27.8 %copy-start.2 = (bf16[768,768]{1,0:T(8,128)(2,1)S(1)}, bf16[768,768]{1,0:T(8,128)(2,1)}, u32[]{:S(2)}) copy-start(bf16[768,768]{1,0:T(8,128)(2,1)} %wk_ref.1) | copy-start | bytes 3538948
